TPU v7x, 128 devices: a whole 4x4x4 slice. The times are simulated.
128 devices in a mesh: grp: 4 (over y_lo, core), hid: 32 (over z, x, y_hi).
Axes of the slice: x: 4, y: 4 (y_hi: 2, y_lo: 2; y = y_hi * 2 + y_lo), z: 4, core: 2. Of those that a mesh axis runs over, the one named last changes fastest.
Arguments:
- states: bfloat16 [8192, 3072], P(('grp', 'hid')), may hold values from -6 to 6
- attention_gain: float32 [3072], replicated, may hold values from 0.1 to 1.9
- forward_gain: float32 [3072], replicated, may hold values from 0.1 to 1.9
- attention_in: float32 [3072, 9216], P('hid'), may hold values from -0.28867513 to 0.28867513
- attention_out: float32 [3072, 3072], P('hid'), may hold values from -0.109375 to 0.109375
- gate_up: float32 [3072, 16384], P('hid'), may hold values from -0.109375 to 0.109375
- down_weight: float32 [8192, 3072], P('hid'), may hold values from -0.0625 to 0.0625
- block_map: int32 [16], replicated, may hold values from 0 to 15, each once
- prompt_lengths: int32 [32], replicated, may hold values from 1 to 32, 640 in all
Outputs:
- hidden_out: bfloat16 [8192, 3072], P(('grp', 'hid'))
- key_cache: bfloat16 [8192, 3072], P('grp', 'hid')
- value_cache: bfloat16 [8192, 3072], P('grp', 'hid')
Inputs may be any that keep to these rules, and one draw needn't show every extreme that they name: block_map is a permutation of the 16 logical blocks. prompt_lengths[p] is the number of used slots of short prompt p.
All inputs are finite; a program needn't handle non-finite values.
Results may differ from a plain program's by a relative error of at most 0.02.
Values may be sent and summed in bfloat16 or wider, within the bound.
A program may use at most 192 MiB of HBM per device.

v0:
```python
import jax
import jax.numpy as jnp
from jax import lax
from jax.sharding import PartitionSpec as P

HD = 96
BLOCK = 512
SHORT_LEN = 32
WINDOW = 4096
SINKS = 4
SHORT_BLOCKS = 2


EPSILON = 1e-05
ROPE_BASE = 10000.0
MASK_FLOOR = -1e30


def rms_norm(values, gain):
    widened = values.astype(jnp.float32)
    scaling = lax.rsqrt(jnp.mean(widened * widened, axis=-1, keepdims=True) + EPSILON)
    return (widened * scaling * gain).astype(jnp.bfloat16)


def rotate(values, positions, head_count, head_size):
    half_size = head_size // 2
    inverse = 1.0 / ROPE_BASE ** (jnp.arange(0, head_size, 2).astype(jnp.float32) / head_size)
    angles = positions.astype(jnp.float32)[:, None] * inverse[None, :]
    cosine = jnp.cos(angles)[:, None, :]
    sine_wave = jnp.sin(angles)[:, None, :]
    shaped = values.reshape(values.shape[0], head_count, head_size)
    first_half = shaped[..., :half_size]
    second_half = shaped[..., half_size:]
    turned = jnp.concatenate(
        [
            first_half * cosine - second_half * sine_wave,
            second_half * cosine + first_half * sine_wave,
        ],
        axis=-1,
    )
    return turned.reshape(values.shape[0], head_count * head_size)


def block_layout(logical, prompt_lengths, long_blocks):
    offset = jnp.arange(BLOCK, dtype=jnp.int32)
    short_pos = offset % SHORT_LEN
    is_long = logical < long_blocks
    positions = jnp.where(is_long, logical * BLOCK + offset, short_pos)
    prompt = (logical - long_blocks) * (BLOCK // SHORT_LEN) + offset // SHORT_LEN
    matches = prompt[:, None] == jnp.arange(prompt_lengths.shape[0], dtype=jnp.int32)[None, :]
    length = jnp.sum(jnp.where(matches, prompt_lengths[None, :], 0), axis=1)
    live_keys = jnp.logical_or(is_long, short_pos < length)
    return (positions, live_keys)


def inverse_map(block_map):
    count_all = block_map.shape[0]
    numbers = jnp.arange(count_all, dtype=jnp.int32)
    matches = block_map[None, :] == numbers[:, None]
    return jnp.sum(jnp.where(matches, numbers[None, :], 0), axis=1)


def attend(queries, key_rows, value_rows, allowed, head_count):
    query_count = queries.shape[0]
    query_heads = queries.reshape(query_count, head_count, HD)
    key_heads = key_rows.reshape(key_rows.shape[0], head_count, HD)
    value_heads = value_rows.reshape(value_rows.shape[0], head_count, HD)
    scores = jnp.einsum(
        "qhd,khd->hqk", query_heads, key_heads, preferred_element_type=jnp.float32
    ) * HD ** (-0.5)
    scores = jnp.where(allowed[None, :, :], scores, MASK_FLOOR)
    row_peak = jnp.max(scores, axis=-1, keepdims=True)
    weights = jnp.exp(scores - row_peak)
    weights = (weights / jnp.sum(weights, axis=-1, keepdims=True)).astype(jnp.bfloat16)
    mixed_heads = jnp.einsum(
        "hqk,khd->qhd", weights, value_heads, preferred_element_type=jnp.float32
    )
    return mixed_heads.reshape(query_count, head_count * HD).astype(jnp.bfloat16)


def attend_slot(
    logical,
    slot_index,
    queries,
    key_all,
    value_all,
    slot_of,
    prompt_lengths,
    long_blocks,
    head_count,
):
    width = key_all.shape[1]
    block_count = key_all.shape[0] // BLOCK
    key_blocks = key_all.reshape(block_count, BLOCK, width)
    value_blocks = value_all.reshape(block_count, BLOCK, width)
    offset = jnp.arange(BLOCK, dtype=jnp.int32)
    span = WINDOW // BLOCK

    def long_branch():
        entries = logical - span + jnp.arange(span + 1, dtype=jnp.int32)
        present = jnp.concatenate([entries >= 0, jnp.ones((1,), jnp.bool_)])
        chosen = jnp.concatenate([jnp.maximum(entries, 0), jnp.zeros((1,), jnp.int32)])
        slot_list = slot_of[chosen]
        picked_keys = key_blocks[slot_list].reshape((span + 2) * BLOCK, width)
        picked_values = value_blocks[slot_list].reshape((span + 2) * BLOCK, width)
        key_pos = (chosen[:, None] * BLOCK + offset[None, :]).reshape(-1)
        is_sink = jnp.repeat(
            jnp.arange(span + 2) == span + 1, BLOCK, total_repeat_length=(span + 2) * BLOCK
        )
        present_flat = jnp.repeat(present, BLOCK, total_repeat_length=(span + 2) * BLOCK)
        query_pos = logical * BLOCK + offset
        in_window = (
            (key_pos[None, :] <= query_pos[:, None])
            & (key_pos[None, :] > query_pos[:, None] - WINDOW)
            & present_flat[None, :]
        )
        as_sink = (key_pos[None, :] < SINKS) & (key_pos[None, :] <= query_pos[:, None] - WINDOW)
        allowed = jnp.where(is_sink[None, :], as_sink, in_window)
        return attend(queries, picked_keys, picked_values, allowed, head_count)

    def short_branch():
        positions, live_keys = block_layout(logical, prompt_lengths, long_blocks)
        own_keys = key_blocks[slot_index]
        own_values = value_blocks[slot_index]
        segment = offset // SHORT_LEN
        allowed = (
            (segment[:, None] == segment[None, :])
            & (positions[None, :] <= positions[:, None])
            & live_keys[None, :]
        )
        return attend(queries, own_keys, own_values, allowed, head_count)

    return lax.cond(logical < long_blocks, long_branch, short_branch)


def body(
    states,
    attention_gain,
    forward_gain,
    attention_in,
    attention_out,
    gate_up,
    down_weight,
    block_map,
    prompt_lengths,
):
    owners = lax.axis_size("hid")
    groups = lax.axis_size("grp")
    rows_dev = states.shape[0]
    group_rows = rows_dev * owners
    per_group = group_rows // BLOCK
    block_count = per_group * groups
    long_blocks = block_count - SHORT_BLOCKS
    model_width = states.shape[1]
    stripe = attention_in.shape[0]
    unit_count = down_weight.shape[0]
    head_count = stripe // HD
    qkv_rows = attention_in.astype(jnp.bfloat16).reshape(stripe, 3, model_width)
    lift_rows = gate_up.astype(jnp.bfloat16).reshape(stripe, 2, gate_up.shape[1] // 2)
    qkv_block, lift_block = (
        lax.all_to_all(qkv_rows, "hid", split_axis=2, concat_axis=0, tiled=True),
        lax.all_to_all(lift_rows, "hid", split_axis=2, concat_axis=0, tiled=True),
    )
    qkv_block = qkv_block.reshape(model_width, 3 * stripe)
    lift_block = lift_block.reshape(model_width, 2 * unit_count)
    out_block = attention_out.astype(jnp.bfloat16)
    down_block = down_weight.astype(jnp.bfloat16)
    rows_all = lax.all_gather(states, "hid", axis=0, tiled=True)
    normed = rms_norm(rows_all, attention_gain)
    joined = jnp.dot(normed, qkv_block, preferred_element_type=jnp.float32)
    group_index = lax.axis_index("grp")
    first_slot = group_index * per_group
    local_map = lax.dynamic_slice_in_dim(block_map, first_slot, per_group)
    positions, _ = jax.vmap(lambda logical: block_layout(logical, prompt_lengths, long_blocks))(
        local_map
    )
    position_flat = positions.reshape(-1)
    queries = rotate(joined[:, :stripe], position_flat, head_count, HD).astype(jnp.bfloat16)
    key_local = rotate(joined[:, stripe : 2 * stripe], position_flat, head_count, HD).astype(
        jnp.bfloat16
    )
    value_local = joined[:, 2 * stripe :].astype(jnp.bfloat16)
    key_all, value_all = (
        lax.all_gather(key_local, "grp", axis=0, tiled=True),
        lax.all_gather(value_local, "grp", axis=0, tiled=True),
    )
    slot_of = inverse_map(block_map)

    def one_block(block_index):
        logical = local_map[block_index]
        query_block = lax.dynamic_slice_in_dim(queries, block_index * BLOCK, BLOCK, 0)
        return attend_slot(
            logical,
            first_slot + block_index,
            query_block,
            key_all,
            value_all,
            slot_of,
            prompt_lengths,
            long_blocks,
            head_count,
        )

    attended = lax.map(one_block, jnp.arange(per_group, dtype=jnp.int32)).reshape(
        group_rows, stripe
    )
    mixed_sum = lax.psum(
        jnp.dot(attended, out_block, preferred_element_type=jnp.float32).astype(jnp.bfloat16), "hid"
    ).astype(jnp.float32)
    residual = rows_all.astype(jnp.float32) + mixed_sum
    normed_two = rms_norm(residual, forward_gain)
    lifted = jnp.dot(normed_two, lift_block, preferred_element_type=jnp.float32)
    activated = (jax.nn.silu(lifted[:, :unit_count]) * lifted[:, unit_count:]).astype(jnp.bfloat16)
    own_residual = lax.dynamic_slice_in_dim(residual, lax.axis_index("hid") * rows_dev, rows_dev, 0)
    forward_sum = lax.psum_scatter(
        jnp.dot(activated, down_block, preferred_element_type=jnp.float32).astype(jnp.bfloat16),
        "hid",
        scatter_dimension=0,
        tiled=True,
    ).astype(jnp.float32)
    hidden_out = (own_residual + forward_sum).astype(jnp.bfloat16)
    return (hidden_out, key_local, value_local)


def solution(mesh):
    in_specs = (
        P(("grp", "hid"), None),
        P(),
        P(),
        P("hid", None),
        P("hid", None),
        P("hid", None),
        P("hid", None),
        P(),
        P(),
    )
    out_specs = (P(("grp", "hid"), None), P("grp", "hid"), P("grp", "hid"))
    return jax.shard_map(body, mesh=mesh, in_specs=in_specs, out_specs=out_specs, check_vma=False)
```

profile of v0, /device:TPU:14, one launch (start us, length us, event | category | flops | bytes accessed | tf_op | source)
XLA Modules:
  0.0 1336.4 jit_solution(5084348465351217150)
XLA Ops:
  7.9 2.2 convert_element_type.95
  10.1 4.0 reshape.473
  14.1 7.1 copy.58
  21.2 10.3 all-to-all-start
  32.9 40.3 %all-to-all-done = bf16[96,3,3072]{0,1,2:T(4,128)(2,1)} async-done(((bf16[96,3,3072]{0,1,2:T(4,128)(2,1)}), bf16[96,3,3072]{0,1,2:T(4,128)(2,1)}, u32[]{:S(2)}, u32[]{:S(2)}) %all-to-all-start) | async-done | bytes 1769504 | tf_op jit(solution)/shard_map/all_to_all | solution.py:161
  73.2 5.3 copy.76
  78.5 4.5 reshape.474
  83.0 85.2 %all-gather.5.cloned.1.call-done = bf16[2048,3072]{1,0:T(8,128)(2,1)} async-done(((bf16[64,3072]{1,0:T(8,128)(2,1)}), bf16[2048,3072]{1,0:T(8,128)(2,1)}) %all-gather.5.cloned.1.call-update) | async-done | bytes 12582928 | tf_op jit(solution)/shard_map/all_gather | solution.py:168
  168.2 7.1 fusion.28
  175.3 7.0 fusion.32
  188.5 19.2 %all-gather.9.cloned.1.call-done = bf16[8192,1,96]{0,2,1:T(8,128)(2,1)} async-done(((bf16[2048,1,96]{0,2,1:T(8,128)(2,1)}), bf16[8192,1,96]{0,2,1:T(8,128)(2,1)}) %all-gather.9.cloned.1.call-update) | async-done | bytes 1572880 | tf_op jit(solution)/shard_map/all_gather | solution.py:184
  207.7 3.1 copy.61
  210.8 24.8 %all-gather.7.cloned.1.call-done = bf16[8192,96]{0,1:T(8,128)(2,1)} async-done(((bf16[2048,96]{0,1:T(8,128)(2,1)}), bf16[8192,96]{0,1:T(8,128)(2,1)}) %all-gather.7.cloned.1.call-update) | async-done | bytes 1572880 | tf_op jit(solution)/shard_map/all_gather | solution.py:185
  235.6 3.8 copy.62
  240.0 154.4 %while.12 = (s32[]{:T(128)}, bf16[4,512,96]{1,2,0:T(8,128)(2,1)}, s32[4]{0:T(128)}, s32[4]{0:T(128)}, bf16[8192,96]{1,0:T(8,128)(2,1)S(1)}, /*index=5*/bf16[8192...) while((s32[]{:T(128)}, bf16[4,512,96]{1,2,0:T(8,128)(2,1)}, ...), condition=%wide.region_10.12_spmd, body=%wide.region_2.11_spmd.sunk | while | flops 1046059136 | bytes 38419620 | solution.py:204
  246.4 5.8 conditional.7
  260.3 38.9 %conditional.7 = (bf16[1,512,96]{1,2,0:T(8,128)(2,1)}) conditional(s32[]{:T(128)} %convert_element_type.156, (s32[]{:T(128)}, s32[]{:T(128)}, bf16[16,512,96]{2,1,0:T(8,128)(2,1)}, s32[512]{0:T(512)S(1)}, s32[]{:T(128)}, /*index=5*/s32[32]{0:T(128)}, bf16[16,512,96]{2,1,0:T(8,128)(2,1)S(1)}, bf16[512,96]{1,0:T(8,128)(2,1)S(1)}) %tuple.104, ...), branch_computations={%region_3.6_spmd, %region_7.10_spmd} | conditional | flops 1046059136 | bytes 37825296
  265.4 2.5 gather_fusion.1
  269.9 7.0 select_select_fusion.1
  279.5 6.5 select_select_fusion
  286.0 8.8 fusion.67
  296.3 2.8 fusion.22
  307.1 38.9 %conditional.7 = (bf16[1,512,96]{1,2,0:T(8,128)(2,1)}) conditional(s32[]{:T(128)} %convert_element_type.156, (s32[]{:T(128)}, s32[]{:T(128)}, bf16[16,512,96]{2,1,0:T(8,128)(2,1)}, s32[512]{0:T(512)S(1)}, s32[]{:T(128)}, /*index=5*/s32[32]{0:T(128)}, bf16[16,512,96]{2,1,0:T(8,128)(2,1)S(1)}, bf16[512,96]{1,0:T(8,128)(2,1)S(1)}) %tuple.104, ...), branch_computations={%region_3.6_spmd, %region_7.10_spmd} | conditional | flops 1046059136 | bytes 37825296
  312.2 2.5 gather_fusion.1
  316.7 7.0 select_select_fusion.1
  326.4 6.5 select_select_fusion
  332.9 8.8 fusion.67
  343.2 2.8 fusion.22
  354.0 38.9 %conditional.7 = (bf16[1,512,96]{1,2,0:T(8,128)(2,1)}) conditional(s32[]{:T(128)} %convert_element_type.156, (s32[]{:T(128)}, s32[]{:T(128)}, bf16[16,512,96]{2,1,0:T(8,128)(2,1)}, s32[512]{0:T(512)S(1)}, s32[]{:T(128)}, /*index=5*/s32[32]{0:T(128)}, bf16[16,512,96]{2,1,0:T(8,128)(2,1)S(1)}, bf16[512,96]{1,0:T(8,128)(2,1)S(1)}) %tuple.104, ...), branch_computations={%region_3.6_spmd, %region_7.10_spmd} | conditional | flops 1046059136 | bytes 37825296
  359.1 2.5 gather_fusion.1
  363.6 7.0 select_select_fusion.1
  373.2 6.5 select_select_fusion
  379.7 8.8 fusion.67
  390.0 2.8 fusion.22
  395.4 7.6 convolution_convert_fusion
  403.1 4.8 convert_element_type.105
  407.9 6.2 reshape.478
  414.0 14.5 %copy.65 = bf16[96,2,8192]{0,1,2:T(2,128)(2,1)} copy(bf16[96,2,8192]{2,1,0:T(2,128)(2,1)} %reshape.478) | data formatting | bytes 6291456 | tf_op jit(solution)/shard_map/reshape | solution.py:159
  428.5 75.9 %all_to_all.30 = bf16[96,2,8192]{0,1,2:T(2,128)(2,1)} all-to-all(bf16[96,2,8192]{0,1,2:T(2,128)(2,1)} %copy.65), channel_id=1, replica_groups=mesh['grp'=4,'hid'=32] {'hid'}, dimensions={2} | all-to-all | bytes 6291456 | tf_op jit(solution)/shard_map/all_to_all | solution.py:162
  504.5 7.8 copy.70
  512.3 5.1 copy.67
  517.4 2.3 copy.74
  519.7 508.1 %all-reduce.2.cloned.1.call-done = bf16[2048,3072]{1,0:T(8,128)(2,1)} async-done(((bf16[2048,3072]{1,0:T(8,128)(2,1)}), bf16[2048,3072]{1,0:T(8,128)(2,1)}) %all-reduce.2.cloned.1.call-update) | async-done | bytes 12582928 | tf_op jit(solution)/shard_map/psum | solution.py:207
  1027.8 19.5 %convert_add_fusion = (f32[2048,3072]{1,0:T(8,128)}, f32[2048]{0:T(1024)S(1)}) fusion(bf16[2048,3072]{1,0:T(8,128)(2,1)} %all-gather.5.cloned.1.call-done, bf16[2048,3072]{1,0:T(8,128)(2,1)} %all-reduce.2.cloned.1.call-done), kind=kLoop, calls=%fused_computation.65 | loop fusion | flops 31455232 | bytes 50339840 | tf_op jit(solution)/shard_map/add | solution.py:210
  1048.5 12.0 fusion.31
  1060.5 11.3 convolution_convert_fusion.1
  1071.8 256.0 %reduce-scatter.2.cloned.1.call-done = bf16[64,3072]{1,0:T(8,128)(2,1)} async-done(((bf16[2048,3072]{1,0:T(8,128)(2,1)}), bf16[64,3072]{1,0:T(8,128)(2,1)}) %reduce-scatter.2.cloned.1.call-update) | async-done | bytes 393232 | tf_op jit(solution)/shard_map/reduce_scatter | solution.py:215
  1327.8 2.1 add_convert_fusion
  (129 shorter events, 64.2 us)
Async XLA Ops:
  7.2 161.0 %all-gather.5.cloned.1.call-start = ((), (), s32[]{:S(2)}) async-start(), calls=%async_computation.3 | async-start | bytes 12976128 | tf_op jit(solution)/shard_map/all_gather | solution.py:168
  21.2 10.4 copy-start.3
  21.2 52.0 %all-to-all-start = ((bf16[96,3,3072]{0,1,2:T(4,128)(2,1)}), bf16[96,3,3072]{0,1,2:T(4,128)(2,1)}, u32[]{:S(2)}, u32[]{:S(2)}) async-start(bf16[96,3,3072]{0,1,2:T(4,128)(2,1)} %copy.58), calls=%async_computation | async-start | bytes 6291456 | tf_op jit(solution)/shard_map/all_to_all | solution.py:161
  31.5 176.2 %all-gather.9.cloned.1.call-start = ((), (), s32[]{:S(2)}) async-start(), calls=%async_computation.7 | async-start | bytes 1966080 | tf_op jit(solution)/shard_map/all_gather | solution.py:184
  83.0 92.3 %copy-start.4 = (f32[3072]{0:T(1024)S(1)}, f32[3072]{0:T(1024)}, u32[]{:S(2)}) copy-start(f32[3072]{0:T(1024)} %param.20) | copy-start | bytes 36868
  182.4 1.9 copy-start.1
  185.3 50.3 %all-gather.7.cloned.1.call-start = ((), (), s32[]{:S(2)}) async-start(), calls=%async_computation.4 | async-start | bytes 1966080 | tf_op jit(solution)/shard_map/all_gather | solution.py:185
  187.3 840.5 %all-reduce.2.cloned.1.call-start = ((), (), s32[]{:S(2)}) async-start(), calls=%async_computation.5 | async-start | bytes 25165824 | tf_op jit(solution)/shard_map/psum | solution.py:207
  262.9 0.6 copy-start.2
  309.8 0.6 copy-start.2
  356.6 0.6 copy-start.2
  403.0 924.8 %reduce-scatter.2.cloned.1.call-start = ((), (), s32[]{:S(2)}) async-start(), calls=%async_computation.6 | async-start | bytes 12976128 | tf_op jit(solution)/shard_map/reduce_scatter | solution.py:215
  519.7 527.6 %copy-start.5 = (f32[3072]{0:T(1024)S(1)}, f32[3072]{0:T(1024)}, u32[]{:S(2)}) copy-start(f32[3072]{0:T(1024)} %param.21) | copy-start | bytes 36868
  1027.8 20.7 %copy-start = (bf16[2048,3072]{1,0:T(8,128)(2,1)S(1)}, bf16[2048,3072]{1,0:T(8,128)(2,1)}, u32[]{:S(2)}) copy-start(bf16[2048,3072]{1,0:T(8,128)(2,1)} %all-reduce.2.cloned.1.call-done) | copy-start | bytes 37748740
Sparse Core Ops, SparseCore 0:
  10.9 157.2 all-gather.4
  185.4 22.1 all-gather.8
  209.9 25.6 all-gather.6
  403.2 624.5 all-reduce.1
  1071.9 255.8 reduce-scatter.1
where the time goes:
time: 1340 us
  waiting for transfers between devices  934 us (70%)
  local copies, waits for them, and re-layouts  114 us (9%)
  other arithmetic  94.2 us (7%)
  blocking collectives  75.9 us (6%)
  matrix products  75.2 us (6%)
  loops' own time  18.3 us (1%)
  between operations  13.9 us (1%)
    psum x1, waiting for transfers between devices, body(): lax.psum(jnp.dot(attended, out_block, preferred_element_type=jnp.float32)...  508 us
    reduce_scatter x1, waiting for transfers between devices, body(): lax.psum_scatter(jnp.dot(activated, down_block, preferred_element_type=jn...  256 us
    all_gather x1, waiting for transfers between devices, body(): rows_all = lax.all_gather(states, 'hid', axis=0, tiled=True)  85.2 us
    all_to_all x1, blocking collectives, body(): lax.all_to_all(lift_rows, 'hid', split_axis=2, concat_axis=0, tiled=True)  75.9 us
    all_to_all x1, waiting for transfers between devices, body(): lax.all_to_all(qkv_rows, 'hid', split_axis=2, concat_axis=0, tiled=True)  40.3 us
    dot_general x4, matrix products, attend(): jnp.einsum('qhd,khd->hqk', query_heads, key_heads, preferred_element_type...  26.9 us
  transfers between devices with their start and end apart: 6, of which 6 were waited for; matrix products, arithmetic and copies ran while one was open for 5% of the time, Pallas kernels for 0%

commit v1 on v0

v1 whole, which is shorter than its diff:
```python
import functools

import jax
import jax.numpy as jnp
import numpy as np
from jax import lax
from jax.experimental import pallas as pl
from jax.experimental.pallas import tpu as pltpu
from jax.sharding import Mesh, PartitionSpec as P

HD = 96
BLOCK = 512
SHORT_LEN = 32
WINDOW = 4096
SINKS = 4
SHORT_BLOCKS = 2
EPSILON = 1e-05
ROPE_BASE = 10000.0
MASK_FLOOR = -1e30
LOG2E = 1.4426950408889634

ROWS = 64
PLANE = ("core", "z", "x")


def rms_norm(values, gain):
    widened = values.astype(jnp.float32)
    scaling = lax.rsqrt(jnp.mean(widened * widened, axis=-1, keepdims=True) + EPSILON)
    return (widened * scaling * gain).astype(jnp.bfloat16)


def inverse_map(block_map):
    numbers = jnp.arange(block_map.shape[0], dtype=jnp.int32)
    matches = block_map[None, :] == numbers[:, None]
    return jnp.sum(jnp.where(matches, numbers[None, :], 0), axis=1)


def attention_kernel(
    own_map, slot_of, half_ref, q_ref, k_ref, v_ref, live_ref, o_ref, m_ref, l_ref, acc_ref
):
    step = pl.program_id(0)
    logical = own_map[step]
    own_half = half_ref[0]
    own_lo = half_ref[1]
    scale = HD ** (-0.5) * LOG2E
    rows = q_ref.shape[1]
    q = q_ref[0]

    row_at = lax.broadcasted_iota(jnp.int32, (rows, 2 * rows), 0)
    col_at = lax.broadcasted_iota(jnp.int32, (rows, 2 * rows), 1)
    row_off = (row_at // ROWS) * (2 * ROWS) + own_half * ROWS + row_at % ROWS
    col_in = col_at % rows
    col_off = (col_in // ROWS) * (2 * ROWS) + (col_at // rows) * ROWS + col_in % ROWS

    def pair(slot):
        low = slot // 8
        inner = slot % 8
        keys = jnp.concatenate([k_ref[low * 16 + inner], k_ref[low * 16 + 8 + inner]], axis=0)
        values = jnp.concatenate([v_ref[low * 16 + inner], v_ref[low * 16 + 8 + inner]], axis=0)
        return keys, values

    def scores_of(keys):
        return (
            lax.dot_general(
                q, keys, (((1,), (1,)), ((), ())), preferred_element_type=jnp.float32
            )
            * scale
        )

    def first(scores, values):
        peak = jnp.max(scores, axis=1, keepdims=True)
        weights = jnp.exp2(scores - peak)
        m_ref[...] = peak
        l_ref[...] = jnp.sum(weights, axis=1, keepdims=True)
        acc_ref[...] = jnp.dot(
            weights.astype(jnp.bfloat16), values, preferred_element_type=jnp.float32
        )

    def more(scores, values):
        old = m_ref[...]
        peak = jnp.maximum(old, jnp.max(scores, axis=1, keepdims=True))
        fade = jnp.exp2(old - peak)
        weights = jnp.exp2(scores - peak)
        m_ref[...] = peak
        l_ref[...] = l_ref[...] * fade + jnp.sum(weights, axis=1, keepdims=True)
        acc_ref[...] = acc_ref[...] * fade + jnp.dot(
            weights.astype(jnp.bfloat16), values, preferred_element_type=jnp.float32
        )

    is_long = logical < slot_of.shape[0] - SHORT_BLOCKS
    own_slot = own_lo * 8 + step

    @pl.when(jnp.logical_not(is_long))
    def _():
        keys, values = pair(own_slot)
        allowed = (row_off // SHORT_LEN == col_off // SHORT_LEN) & (col_off <= row_off)
        allowed = allowed & (live_ref[0] > 0.0)
        first(jnp.where(allowed, scores_of(keys), MASK_FLOOR), values)

    @pl.when(is_long)
    def _():
        keys, values = pair(own_slot)
        first(jnp.where(col_off <= row_off, scores_of(keys), MASK_FLOOR), values)
        span = WINDOW // BLOCK
        oldest = jnp.maximum(logical - span + 1, 0)

        def whole(index, carry):
            keys, values = pair(slot_of[index])
            more(scores_of(keys), values)
            return carry

        lax.fori_loop(oldest, logical, whole, 0)

        @pl.when(logical >= span)
        def _():
            edge = logical - span
            keys, values = pair(slot_of[edge])
            allowed = (col_off > row_off) | (edge * BLOCK + col_off < SINKS)
            more(jnp.where(allowed, scores_of(keys), MASK_FLOOR), values)

        @pl.when(logical > span)
        def _():
            slot = slot_of[0]
            at = (slot // 8) * 16 + slot % 8
            keys = k_ref[at, 0:128]
            values = v_ref[at, 0:128]
            allowed = lax.broadcasted_iota(jnp.int32, (rows, 128), 1) < SINKS
            more(jnp.where(allowed, scores_of(keys), MASK_FLOOR), values)

    o_ref[0] = (acc_ref[...] / l_ref[...]).astype(jnp.bfloat16)


def attention(q, k_all, v_all, own_map, slot_of, places, live):
    slots, rows, _ = q.shape
    return pl.pallas_call(
        attention_kernel,
        grid_spec=pltpu.PrefetchScalarGridSpec(
            num_scalar_prefetch=3,
            grid=(slots,),
            in_specs=[
                pl.BlockSpec((1, rows, HD), lambda i, *_: (i, 0, 0)),
                pl.BlockSpec(k_all.shape, lambda i, *_: (0, 0, 0)),
                pl.BlockSpec(v_all.shape, lambda i, *_: (0, 0, 0)),
                pl.BlockSpec((1, 1, 2 * rows), lambda i, *_: (i, 0, 0)),
            ],
            out_specs=pl.BlockSpec((1, rows, HD), lambda i, *_: (i, 0, 0)),
            scratch_shapes=[
                pltpu.VMEM((rows, 1), jnp.float32),
                pltpu.VMEM((rows, 1), jnp.float32),
                pltpu.VMEM((rows, HD), jnp.float32),
            ],
        ),
        out_shape=jax.ShapeDtypeStruct(q.shape, jnp.bfloat16),
        cost_estimate=pl.CostEstimate(
            flops=8_000_000_000, bytes_accessed=8_000_000, transcendentals=8_000_000
        ),
        name="attention",
    )(own_map, slot_of, places, q, k_all, v_all, live)


def rope_tables(positions):
    inverse = 1.0 / ROPE_BASE ** (jnp.arange(0, HD, 2).astype(jnp.float32) / HD)
    angles = positions.astype(jnp.float32)[:, None] * inverse[None, :]
    return jnp.cos(angles), jnp.sin(angles)


def rotate(values, cosine, sine):
    half = HD // 2
    one, two = values[:, :half], values[:, half:]
    return jnp.concatenate(
        [one * cosine - two * sine, two * cosine + one * sine], axis=-1
    ).astype(jnp.bfloat16)


def body(
    states,
    attention_gain,
    forward_gain,
    attention_in,
    attention_out,
    gate_up,
    down_weight,
    block_map,
    prompt_lengths,
):
    width = states.shape[1]
    units = down_weight.shape[0]
    core = lax.axis_index("core")
    y_hi = lax.axis_index("y_hi")
    y_lo = lax.axis_index("y_lo")
    blocks = block_map.shape[0]
    long_blocks = blocks - SHORT_BLOCKS
    rows = 32 * ROWS

    flip = [
        (((a * 2 + c) * 2 + b), (((1 - a) * 2 + c) * 2 + (1 - b)))
        for a in range(2)
        for c in range(2)
        for b in range(2)
    ]
    swap = [
        (((a * 2 + c) * 2 + b), (((1 - a) * 2 + (1 - c)) * 2 + (1 - b)))
        for a in range(2)
        for c in range(2)
        for b in range(2)
        if b != c
    ]

    qkv = attention_in.astype(jnp.bfloat16).reshape(HD, 3, 16, 2, HD)
    gu = gate_up.astype(jnp.bfloat16).reshape(HD, 2, 16, 2, units)

    def spread(full):
        mine = lax.dynamic_index_in_dim(full, core, 3, keepdims=False)
        other = lax.ppermute(mine, ("y_lo", "core", "y_hi"), flip)
        zero = jnp.where(y_hi == 0, mine, other)
        one = jnp.where(y_hi == 0, other, mine)
        both = jnp.stack([zero, one], axis=0)
        both = jnp.transpose(both, (3, 0, 1, 2, 4))
        got = lax.all_to_all(both, ("z", "x"), split_axis=0, concat_axis=0, tiled=True)
        return got.reshape(width, -1)

    def own(shard):
        narrow = shard.astype(jnp.bfloat16)
        other = lax.ppermute(narrow, ("y_lo", "core", "y_hi"), swap)
        return jnp.where(y_hi == core, narrow, other)

    w_qkv = spread(qkv)
    w_gu = spread(gu)
    w_out = own(attention_out)
    w_down = own(down_weight)

    normed = lax.all_gather(rms_norm(states, attention_gain), PLANE, axis=0, tiled=True)
    joined = jnp.dot(normed, w_qkv, preferred_element_type=jnp.float32)

    own_map = lax.dynamic_slice_in_dim(block_map, y_lo * 8, 8)
    at = jnp.arange(256, dtype=jnp.int32)
    at = (at // ROWS) * (2 * ROWS) + at % ROWS
    offset = at + y_hi * ROWS
    positions = jnp.where(
        own_map[:, None] < long_blocks, own_map[:, None] * BLOCK + offset[None], offset % SHORT_LEN
    ).reshape(-1)
    cosine, sine = rope_tables(positions)
    q = rotate(joined[:, :HD], cosine, sine)
    k = rotate(joined[:, HD : 2 * HD], cosine, sine)
    v = joined[:, 2 * HD :].astype(jnp.bfloat16)
    kv = jnp.stack([k, v])
    kv_all = lax.all_gather(kv, ("y_lo", "y_hi"), axis=1)
    kv_all = kv_all.reshape(2, 32, 256, HD)

    offsets = jnp.concatenate([at, at + ROWS])
    prompt = (own_map - long_blocks)[:, None] * (BLOCK // SHORT_LEN) + offsets[None] // SHORT_LEN
    matches = prompt[:, :, None] == jnp.arange(prompt_lengths.shape[0], dtype=jnp.int32)
    length = jnp.sum(jnp.where(matches, prompt_lengths, 0), axis=2)
    live = (offsets[None] % SHORT_LEN < length).astype(jnp.float32)[:, None, :]

    places = jnp.stack([y_hi, y_lo]).astype(jnp.int32)
    attended = attention(
        q.reshape(8, 256, HD), kv_all[0], kv_all[1], own_map, inverse_map(block_map), places, live
    ).reshape(rows, HD)

    group = lax.dynamic_index_in_dim(kv_all.reshape(2, 2, 2, 2, 4, 4, ROWS, HD), y_lo, 1, False)

    def cache_rows(target):
        picked = lax.dynamic_index_in_dim(group, target, 2, False)
        return jnp.transpose(picked, (0, 2, 3, 1, 4, 5)).reshape(2, rows, HD)

    partner = lax.ppermute(
        cache_rows(1 - core),
        ("core", "y_hi"),
        [(b * 2 + b, (1 - b) * 2 + b) for b in range(2)],
    )
    cache = jnp.where(core == y_hi, cache_rows(core), partner)

    def scatter(left, right):
        partial = jnp.dot(left, right, preferred_element_type=jnp.float32).astype(jnp.bfloat16)
        return lax.psum_scatter(partial, PLANE, scatter_dimension=0, tiled=True).astype(
            jnp.float32
        )

    residual = states.astype(jnp.float32) + scatter(attended, w_out)
    normed_two = lax.all_gather(rms_norm(residual, forward_gain), PLANE, axis=0, tiled=True)
    lifted = jnp.dot(normed_two, w_gu, preferred_element_type=jnp.float32)
    activated = (jax.nn.silu(lifted[:, :units]) * lifted[:, units:]).astype(jnp.bfloat16)
    hidden_out = (residual + scatter(activated, w_down)).astype(jnp.bfloat16)
    return (hidden_out, cache[0], cache[1])


def solution(mesh):
    fine = Mesh(mesh.devices.reshape(2, 2, 4, 4, 2), ("y_lo", "core", "z", "x", "y_hi"))
    hid = ("z", "x", "y_hi")
    grp = ("y_lo", "core")
    in_specs = (
        P(grp + hid, None),
        P(),
        P(),
        P(hid, None),
        P(hid, None),
        P(hid, None),
        P(hid, None),
        P(),
        P(),
    )
    out_specs = (P(grp + hid, None), P(grp, hid), P(grp, hid))
    return jax.shard_map(
        body, mesh=fine, in_specs=in_specs, out_specs=out_specs, check_vma=False
    )
```

time: 1340 us -> 580 us (0.43)
  waiting for transfers between devices: 934 us -> 391 us
  blocking collectives: 75.9 us -> 0 us
  other arithmetic: 94.2 us -> 28.3 us
  local copies, waits for them, and re-layouts: 114 us -> 56.1 us
  matrix products: 75.2 us -> 34.4 us
  Pallas kernels: 0 us -> 30.9 us
  loops' own time: 18.3 us -> 0 us
    psum x1 -> x0, waiting for transfers between devices: 508 us -> none  [body(): lax.psum(jnp.dot(attended, out_block, preferred_element_type=jnp.float32)...]
    all_to_all x1 -> x0, blocking collectives: 75.9 us -> none  [body(): lax.all_to_all(lift_rows, 'hid', split_axis=2, concat_axis=0, tiled=True)]
    all_gather x3, waiting for transfers between devices: 129 us -> 59.7 us  [the longest x1 59.7 us: body(): kv_all = lax.all_gather(kv, ('y_lo', 'y_hi'), axis=1)]
    ppermute x0 -> x5, waiting for transfers between devices: none -> 60.5 us  [the longest x2 59 us: spread(): other = lax.ppermute(mine, ('y_lo', 'core', 'y_hi'), flip)]
    reduce_scatter x1 -> x2, waiting for transfers between devices: 256 us -> 199 us  [scatter(): lax.psum_scatter(partial, PLANE, scatter_dimension=0, tiled=True)]
    dot_general x12 -> x4, matrix products: 75.2 us -> 34.4 us  [the longest x2 17 us: scatter(): jnp.dot(left, right, preferred_element_type=jnp.float32)]
    gather x12 -> x0, other arithmetic: 40.5 us -> none  [the longest x3 21 us: long_branch(): jnp.repeat(jnp.arange(span + 2) == span + 1, BLOCK, total_repeat_length=(...]
    all_to_all x1 -> x2, waiting for transfers between devices: 40.3 us -> 71.6 us  [spread(): lax.all_to_all(both, ('z', 'x'), split_axis=0, concat_axis=0, tiled=True)]
  transfers between devices with their start and end apart: 6 -> 12, of which waited for: 6 -> 8; matrix products, arithmetic and copies ran while one was open for 5% -> 14% of each run, Pallas kernels for 0% -> 5%
where the time goes in v1:
time: 580 us; the launch traced here: 579 us
  waiting for transfers between devices  391 us (67%)
  local copies, waits for them, and re-layouts  56.1 us (10%)
  matrix products  34.4 us (6%)
  Pallas kernels  30.9 us (5%)
  other arithmetic  28.3 us (5%)
  starting transfers between devices  23.7 us (4%)
  between operations  14.1 us (2%)
    reduce_scatter x2, waiting for transfers between devices, scatter(): lax.psum_scatter(partial, PLANE, scatter_dimension=0, tiled=True)  199 us
    all_to_all x2, waiting for transfers between devices, spread(): lax.all_to_all(both, ('z', 'x'), split_axis=0, concat_axis=0, tiled=True)  71.6 us
    all_gather x1, waiting for transfers between devices, body(): kv_all = lax.all_gather(kv, ('y_lo', 'y_hi'), axis=1)  59.7 us
    ppermute x2, waiting for transfers between devices, spread(): other = lax.ppermute(mine, ('y_lo', 'core', 'y_hi'), flip)  59 us
    pallas_call x1, Pallas kernels, attention(): pl.pallas_call(attention_kernel, grid_spec=pltpu.PrefetchScalarGridSpec(n...  30.9 us
    dot_general x2, matrix products, scatter(): jnp.dot(left, right, preferred_element_type=jnp.float32)  17 us
    all_to_all x2, starting transfers between devices, spread(): lax.all_to_all(both, ('z', 'x'), split_axis=0, concat_axis=0, tiled=True)  14.5 us
  transfers between devices with their start and end apart: 12, of which 8 were waited for; matrix products, arithmetic and copies ran while one was open for 14% of the time, Pallas kernels for 5%

profile of v1, /device:TPU:14, one launch (start us, length us, event | category | flops | bytes accessed | tf_op | source)
XLA Modules:
  0.0 578.8 jit_solution(11817048123040649710)
XLA Ops:
  7.2 1.2 fusion.5
  8.4 1.9 fusion.7
  10.3 2.2 convert_element_type.80
  12.5 3.4 reshape.322
  16.0 4.1 constant_dynamic-slice_fusion.1
  20.2 1.7 collective-permute-start
  21.9 26.2 %collective-permute-done = bf16[96,3,16,96]{3,2,1,0:T(8,128)(2,1)} collective-permute-done((bf16[96,3,16,96]{3,2,1,0:T(8,128)(2,1)S(1)}, bf16[96,3,16,96]{3,2,1,0:T(8,128)(2,1)}, u32[]{:S(2)}, u32[]{:S(2)}) %collective-permute-start) | collective-permute-done | bytes 884768 | tf_op jit(solution)/shard_map/ppermute | solution.py:214
  48.1 1.5 select_bitcast_fusion.3
  50.1 2.0 copy.66
  52.1 8.5 %all-to-all-start = ((bf16[16,2,96,3,96]{4,2,3,1,0:T(8,128)(2,1)}), bf16[16,2,96,3,96]{4,2,3,1,0:T(8,128)(2,1)S(1)}, u32[]{:S(2)}, u32[]{:S(2)}) async-start(bf16[16,2,96,3,96]{4,2,3,1,0:T(8,128)(2,1)} %copy.66), calls=%async_computation | async-start | bytes 4718592 | tf_op jit(solution)/shard_map/all_to_all | solution.py:219
  60.9 40.1 %all-to-all-done = bf16[16,2,96,3,96]{4,2,3,1,0:T(8,128)(2,1)S(1)} async-done(((bf16[16,2,96,3,96]{4,2,3,1,0:T(8,128)(2,1)}), bf16[16,2,96,3,96]{4,2,3,1,0:T(8,128)(2,1)S(1)}, u32[]{:S(2)}, u32[]{:S(2)}) %all-to-all-start) | async-done | bytes 1769504 | tf_op jit(solution)/shard_map/all_to_all | solution.py:219
  101.1 4.1 copy.67
  105.1 7.0 %reshape.323 = bf16[3072,288]{0,1:T(8,128)(2,1)S(1)} reshape(bf16[16,2,96,3,96]{2,1,0,4,3:T(2,128)(2,1)} %copy.67) | data formatting | bytes 3538944 | tf_op jit(solution)/shard_map/reshape | solution.py:220
  112.2 6.9 %fusion.37 = f32[2048,288]{0,1:T(8,128)S(1)} fusion(bf16[2048,3072]{1,0:T(8,128)(2,1)} %all-gather.5.cloned.1.call-done, bf16[3072,288]{0,1:T(8,128)(2,1)S(1)} %reshape.323), kind=kOutput, calls=%fused_computation.97 | convolution fusion | flops 3623878656 | bytes 16711680 | tf_op jit(solution)/shard_map/dot_general | solution.py:233
  119.1 1.8 fusion.28
  122.9 1.5 collective-permute-start.1
  127.1 1.1 pad_maximum_fusion.1.q_ref
  128.2 59.7 %all-gather.9.cloned.1.call-done = bf16[2,8192,96]{1,2,0:T(8,128)(2,1)} async-done(((bf16[2,2048,96]{1,2,0:T(8,128)(2,1)}), bf16[2,8192,96]{1,2,0:T(8,128)(2,1)}) %all-gather.9.cloned.1.call-update) | async-done | bytes 3145744 | tf_op jit(solution)/shard_map/all_gather | solution.py:247
  187.9 2.1 fusion.36
  190.0 2.4 copy.70
  192.4 2.4 copy.71
  194.8 30.9 %attention.1 = bf16[8,256,96]{2,1,0:T(8,128)(2,1)} custom-call(s32[8]{0:T(128)} %copy-done.7, s32[16]{0:T(128)} %select_reduce_fusion.1.slot_of, s32[2]{0:T(128)} %pad_add_fusion.1.half_ref, bf16[8,256,96]{2,1,0:T(8,128)(2,1)} %pad_maximum_fusion.1.q_ref, bf16[32,256,96]{2,1,0:T(8,128)(2,1)} %bitcast.68, bf16[32,256,96]{2,1,0:T(8,128)(2,1)} %bitcast.69, ...), custom_call_target="tpu_custom_call" | custom-call | flops 8000000000 | bytes 8000000 | tf_op jit(solution)/shard_map/attention/pallas_call | solution.py:135
  225.7 9.2 %convolution_convert_fusion = bf16[2048,3072]{1,0:T(8,128)(2,1)} fusion(bf16[2048,96]{1,0:T(8,128)(2,1)} %bitcast.74, bf16[96,3072]{1,0:T(8,128)(2,1)} %convert_element_type.85, bf16[96,3072]{1,0:T(8,128)(2,1)} %collective-permute-done.1, pred[]{:T(512)S(6)} %eq.51), kind=kOutput, calls=%fused_computation | convolution fusion | flops 1214545920 | bytes 14155777 | tf_op jit(solution)/shard_map/dot_general | solution.py:275
  235.0 108.6 %reduce-scatter.3.cloned.1.call-done = bf16[64,3072]{1,0:T(8,128)(2,1)} async-done(((bf16[2048,3072]{1,0:T(8,128)(2,1)}), bf16[64,3072]{1,0:T(8,128)(2,1)}) %reduce-scatter.3.cloned.1.call-update) | async-done | bytes 393232 | tf_op jit(solution)/shard_map/reduce_scatter | solution.py:276
  343.6 1.2 multiply_reduce_fusion
  344.8 1.9 multiply_convert_fusion
  346.7 4.8 convert_element_type.89
  351.5 4.8 reshape.325
  356.3 3.7 constant_dynamic-slice_fusion
  360.5 1.8 collective-permute-start.2
  362.3 32.7 %collective-permute-done.2 = bf16[96,2,16,256]{3,2,1,0:T(8,128)(2,1)S(1)} collective-permute-done((bf16[96,2,16,256]{3,2,1,0:T(8,128)(2,1)S(1)}, bf16[96,2,16,256]{3,2,1,0:T(8,128)(2,1)S(1)}, u32[]{:S(2)}, u32[]{:S(2)}) %collective-permute-start.2) | collective-permute-done | bytes 1572896 | tf_op jit(solution)/shard_map/ppermute | solution.py:214
  395.6 4.9 copy.72
  400.5 6.0 %all-to-all-start.1 = ((bf16[16,2,96,2,256]{4,3,2,1,0:T(2,128)(2,1)}), bf16[16,2,96,2,256]{4,3,2,1,0:T(2,128)(2,1)S(1)}, u32[]{:S(2)}, u32[]{:S(2)}) async-start(bf16[16,2,96,2,256]{4,3,2,1,0:T(2,128)(2,1)} %copy.72), calls=%async_computation.2 | async-start | bytes 6291456 | tf_op jit(solution)/shard_map/all_to_all | solution.py:219
  406.6 3.3 convert_element_type.91
  409.9 1.9 collective-permute-start.3
  411.7 31.5 %all-to-all-done.1 = bf16[16,2,96,2,256]{4,3,2,1,0:T(2,128)(2,1)S(1)} async-done(((bf16[16,2,96,2,256]{4,3,2,1,0:T(2,128)(2,1)}), bf16[16,2,96,2,256]{4,3,2,1,0:T(2,128)(2,1)S(1)}, u32[]{:S(2)}, u32[]{:S(2)}) %all-to-all-start.1) | async-done | bytes 3145760 | tf_op jit(solution)/shard_map/all_to_all | solution.py:219
  443.2 2.2 copy.83
  445.4 10.5 %fusion.38 = f32[2048,512]{1,0:T(8,128)S(1)} fusion(bf16[2048,3072]{1,0:T(8,128)(2,1)} %all-gather.7.cloned.1.call-done, bf16[3072,512]{1,0:T(8,128)(2,1)} %bitcast.67), kind=kOutput, calls=%fused_computation.98 | convolution fusion | flops 6442450944 | bytes 19922944 | tf_op jit(solution)/shard_map/dot_general | solution.py:282
  456.0 7.8 %convolution_convert_fusion.1 = bf16[2048,3072]{1,0:T(8,128)(2,1)} fusion(bf16[256,3072]{1,0:T(8,128)(2,1)} %convert_element_type.91, bf16[256,3072]{1,0:T(8,128)(2,1)} %collective-permute-done.3, pred[]{:T(512)S(6)} %eq.51, f32[2048,512]{1,0:T(8,128)S(1)} %fusion.38), kind=kOutput, calls=%fused_computation.1 | convolution fusion | flops 3231449088 | bytes 19922944 | tf_op jit(solution)/shard_map/dot_general | solution.py:275
  463.9 1.8 copy-done
  465.7 3.9 copy.73
  469.6 1.7 dynamic-slice_bitcast_fusion.1
  472.0 2.2 collective-permute-start.4
  474.3 1.5 collective-permute-done.4
  475.8 1.6 copy.77
  477.7 1.0 copy.78
  479.6 90.8 %reduce-scatter.5.cloned.1.call-done = bf16[64,3072]{1,0:T(8,128)(2,1)} async-done(((bf16[2048,3072]{1,0:T(8,128)(2,1)}), bf16[64,3072]{1,0:T(8,128)(2,1)}) %reduce-scatter.5.cloned.1.call-update) | async-done | bytes 393232 | tf_op jit(solution)/shard_map/reduce_scatter | solution.py:276
  570.4 1.9 add_convert_fusion
  (61 shorter events, 8.8 us)
Async XLA Ops:
  7.2 105.0 %all-gather.5.cloned.1.call-start = ((), (), s32[]{:S(2)}) async-start(), calls=%async_computation.4 | async-start | bytes 12976128 | tf_op jit(solution)/shard_map/all_gather | solution.py:232
  20.2 27.9 %collective-permute-start = (bf16[96,3,16,96]{3,2,1,0:T(8,128)(2,1)S(1)}, bf16[96,3,16,96]{3,2,1,0:T(8,128)(2,1)}, u32[]{:S(2)}, u32[]{:S(2)}) collective-permute-start(bf16[96,3,16,96]{3,2,1,0:T(8,128)(2,1)S(1)} %bitcast.73), channel_id=1, source_target_pairs={{0,65},{1,64},{32,97},{33,96},{64,1},{65,0},{96,33},{97,32},{2,67}... | collective-permute-start | bytes 2654216 | tf_op jit(solution)/shard_map/ppermute | solution.py:214
  52.1 8.6 %copy-start.6 = (s32[16]{0:T(128)S(1)}, s32[16]{0:T(128)}, u32[]{:S(2)}) copy-start(s32[16]{0:T(128)} %param.16) | copy-start | bytes 196
  52.1 48.9 %all-to-all-start = ((bf16[16,2,96,3,96]{4,2,3,1,0:T(8,128)(2,1)}), bf16[16,2,96,3,96]{4,2,3,1,0:T(8,128)(2,1)S(1)}, u32[]{:S(2)}, u32[]{:S(2)}) async-start(bf16[16,2,96,3,96]{4,2,3,1,0:T(8,128)(2,1)} %copy.66), calls=%async_computation | async-start | bytes 4718592 | tf_op jit(solution)/shard_map/all_to_all | solution.py:219
  60.7 127.2 %all-gather.9.cloned.1.call-start = ((), (), s32[]{:S(2)}) async-start(), calls=%async_computation.8 | async-start | bytes 3932160 | tf_op jit(solution)/shard_map/all_gather | solution.py:247
  60.8 44.3 %copy-start.7 = (s32[8]{0:T(128)}, s32[8]{0:T(128)S(1)}, u32[]{:S(2)}) copy-start(s32[8]{0:T(128)S(1)} %get-tuple-element.19.own_map) | copy-start | bytes 100
  119.1 2.9 copy-start.3
  120.9 4.9 copy-start.5
  121.9 221.7 %reduce-scatter.3.cloned.1.call-start = ((), (), s32[]{:S(2)}) async-start(), calls=%async_computation.5 | async-start | bytes 12976128 | tf_op jit(solution)/shard_map/reduce_scatter | solution.py:276
  122.9 102.9 %collective-permute-start.1 = (bf16[96,3072]{1,0:T(8,128)(2,1)}, bf16[96,3072]{1,0:T(8,128)(2,1)}, u32[]{:S(2)}, u32[]{:S(2)}) collective-permute-start(bf16[96,3072]{1,0:T(8,128)(2,1)} %convert_element_type.85), channel_id=1, source_target_pairs={{1,96},{32,65},{65,32},{96,1},{3,98},{34,67},{67,34},{98,3},{5,100... | collective-permute-start | bytes 1769480 | tf_op jit(solution)/shard_map/ppermute | solution.py:224
  234.9 108.7 %copy-start.1 = (bf16[64,3072]{1,0:T(8,128)(2,1)S(1)}, bf16[64,3072]{1,0:T(8,128)(2,1)}, u32[]{:S(2)}) copy-start(bf16[64,3072]{1,0:T(8,128)(2,1)} %param.9) | copy-start | bytes 1179652
  234.9 109.9 %copy-start.4 = (f32[3072]{0:T(1024)S(1)}, f32[3072]{0:T(1024)}, u32[]{:S(2)}) copy-start(f32[3072]{0:T(1024)} %param.11) | copy-start | bytes 36868
  234.9 210.5 %all-gather.7.cloned.1.call-start = ((), (), s32[]{:S(2)}) async-start(), calls=%async_computation.6 | async-start | bytes 12976128 | tf_op jit(solution)/shard_map/all_gather | solution.py:281
  360.5 34.5 %collective-permute-start.2 = (bf16[96,2,16,256]{3,2,1,0:T(8,128)(2,1)S(1)}, bf16[96,2,16,256]{3,2,1,0:T(8,128)(2,1)S(1)}, u32[]{:S(2)}, u32[]{:S(2)}) collective-permute-start(bf16[96,2,16,256]{3,2,1,0:T(8,128)(2,1)S(1)} %bitcast.72), channel_id=1, source_target_pairs={{0,65},{1,64},{32,97},{33,96},{64,1},{65,0},{96,33},{97,32},{2,67}... | collective-permute-start | bytes 4718600 | tf_op jit(solution)/shard_map/ppermute | solution.py:214
  400.5 42.7 %all-to-all-start.1 = ((bf16[16,2,96,2,256]{4,3,2,1,0:T(2,128)(2,1)}), bf16[16,2,96,2,256]{4,3,2,1,0:T(2,128)(2,1)S(1)}, u32[]{:S(2)}, u32[]{:S(2)}) async-start(bf16[16,2,96,2,256]{4,3,2,1,0:T(2,128)(2,1)} %copy.72), calls=%async_computation.2 | async-start | bytes 6291456 | tf_op jit(solution)/shard_map/all_to_all | solution.py:219
  406.6 163.9 %reduce-scatter.5.cloned.1.call-start = ((), (), s32[]{:S(2)}) async-start(), calls=%async_computation.7 | async-start | bytes 12976128 | tf_op jit(solution)/shard_map/reduce_scatter | solution.py:276
  409.9 46.1 %collective-permute-start.3 = (bf16[256,3072]{1,0:T(8,128)(2,1)}, bf16[256,3072]{1,0:T(8,128)(2,1)}, u32[]{:S(2)}, u32[]{:S(2)}) collective-permute-start(bf16[256,3072]{1,0:T(8,128)(2,1)} %convert_element_type.91), channel_id=1, source_target_pairs={{1,96},{32,65},{65,32},{96,1},{3,98},{34,67},{67,34},{98,3},{5,100... | collective-permute-start | bytes 4718600 | tf_op jit(solution)/shard_map/ppermute | solution.py:224
  463.8 1.9 copy-start
  472.0 3.9 collective-permute-start.4
  477.6 92.8 %copy-start.2 = (bf16[64,3072]{1,0:T(8,128)(2,1)S(1)}, bf16[64,3072]{1,0:T(8,128)(2,1)}, u32[]{:S(2)}) copy-start(bf16[64,3072]{1,0:T(8,128)(2,1)} %reduce-scatter.3.cloned.1.call-done) | copy-start | bytes 1179652
Sparse Core Ops, SparseCore 0:
  10.8 90.4 all-gather.4
  122.0 65.8 all-gather.8
  235.1 108.4 reduce-scatter.2
  346.9 62.7 all-gather.6
  464.0 106.3 reduce-scatter.4

commit v2 on v1

--- a/solution.py
+++ b/solution.py
@@ -158,6 +158,464 @@
     )(own_map, slot_of, places, q, k_all, v_all, live)
 
 
+MESH = pl.DeviceIdType.MESH
+HALF = ROWS // 2
+
+
+def ring(axis):
+    me = lax.axis_index(axis)
+    return me, lax.rem(me + 1, 4), lax.rem(me + 3, 4), lax.rem(me + 2, 4)
+
+
+def meet():
+    barrier = pltpu.get_barrier_semaphore()
+    for axis in ("x", "z"):
+        _, right, left, _ = ring(axis)
+        for peer in (right, left):
+            pl.semaphore_signal(barrier, inc=1, device_id={axis: peer}, device_id_type=MESH)
+    pl.semaphore_signal(
+        barrier, inc=1, device_id={"core": 1 - lax.axis_index("core")}, device_id_type=MESH
+    )
+    pl.semaphore_wait(barrier, 5)
+
+
+def push(src, dst, sems, at, axis, peer):
+    send, recv = sems
+    return pltpu.make_async_remote_copy(
+        src_ref=src,
+        dst_ref=dst,
+        send_sem=send.at[at],
+        recv_sem=recv.at[at],
+        device_id={axis: peer},
+        device_id_type=MESH,
+    )
+
+
+def scatter_steps(
+    make, other, held, near, early, late, early_two, late_two, total, sems, finish
+):
+    core = lax.axis_index("core")
+    rings = (ring("z"), ring("x"))
+    axes = ("z", "x")
+    copies = []
+
+    def go(copy):
+        copy.start()
+        copies.append(copy)
+        return copy
+
+    def big_at(half, step):
+        me, right, left, far = rings[half]
+        return (far, right, left, me)[step]
+
+    swaps = {}
+    for step in range(4):
+        for half in range(2):
+            at = half * 4 + step
+            make(other.at[half, step], None, half, 1 - core, big_at(half, step))
+            swaps[half, step] = go(
+                push(
+                    other.at[half, step],
+                    near.at[half, step],
+                    sems[0],
+                    at,
+                    "core",
+                    1 - core,
+                )
+            )
+
+    first = {}
+    second = {}
+    for half in range(2):
+        _, right, left, _ = rings[half]
+        swaps[half, 0].wait_recv()
+        make(held.at[half, 0], near.at[half, 0], half, core, big_at(half, 0))
+        for side, peer in ((0, right), (1, left)):
+            first[half, side] = go(
+                push(
+                    held.at[half, 0, pl.ds(2 * side, 2)],
+                    early.at[half, side],
+                    sems[1],
+                    half * 2 + side,
+                    axes[half],
+                    peer,
+                )
+            )
+    for side in range(2):
+        for half in range(2):
+            _, right, left, _ = rings[half]
+            step = 1 + side
+            swaps[half, step].wait_recv()
+            make(held.at[half, step], near.at[half, step], half, core, big_at(half, step))
+            first[half, side].wait_recv()
+            part = held.at[half, step, pl.ds(2 * side, 2)]
+            part[...] = (
+                part[...].astype(jnp.float32) + early[half, side].astype(jnp.float32)
+            ).astype(jnp.bfloat16)
+            second[half, side] = go(
+                push(
+                    held.at[half, step],
+                    late.at[half, side],
+                    sems[2],
+                    half * 2 + side,
+                    axes[half],
+                    (right, left)[side],
+                )
+            )
+    for half in range(2):
+        swaps[half, 3].wait_recv()
+        make(held.at[half, 3], near.at[half, 3], half, core, big_at(half, 3))
+
+    def small_at(half, step):
+        me, right, left, far = rings[1 - half]
+        return (far, right, left, me)[step]
+
+    third = {}
+    fourth = {}
+
+    def gather_small(half, step):
+        at = small_at(half, step)
+        total[half, step] = (
+            held[half, 3, at].astype(jnp.float32)
+            + late[half, 0, at].astype(jnp.float32)
+            + late[half, 1, at].astype(jnp.float32)
+        ).astype(jnp.bfloat16)
+
+    for half in range(2):
+        _, right, left, _ = rings[1 - half]
+        for side in range(2):
+            second[half, side].wait_recv()
+        gather_small(half, 0)
+        for side, peer in ((0, right), (1, left)):
+            third[half, side] = go(
+                push(
+                    total.at[half, 0, pl.ds(16 * side, 16)],
+                    early_two.at[half, side],
+                    sems[3],
+                    half * 2 + side,
+                    axes[1 - half],
+                    peer,
+                )
+            )
+        gather_small(half, 1)
+        gather_small(half, 2)
+    for side in range(2):
+        for half in range(2):
+            _, right, left, _ = rings[1 - half]
+            third[half, side].wait_recv()
+            part = total.at[half, 1 + side, pl.ds(16 * side, 16)]
+            part[...] = (
+                part[...].astype(jnp.float32) + early_two[half, side].astype(jnp.float32)
+            ).astype(jnp.bfloat16)
+            fourth[half, side] = go(
+                push(
+                    total.at[half, 1 + side],
+                    late_two.at[half, side],
+                    sems[4],
+                    half * 2 + side,
+                    axes[1 - half],
+                    (right, left)[side],
+                )
+            )
+    for half in range(2):
+        at = small_at(half, 3)
+        for side in range(2):
+            fourth[half, side].wait_recv()
+        finish(
+            half,
+            held[half, 3, at].astype(jnp.float32)
+            + late[half, 0, at].astype(jnp.float32)
+            + late[half, 1, at].astype(jnp.float32)
+            + late_two[half, 0].astype(jnp.float32)
+            + late_two[half, 1].astype(jnp.float32),
+        )
+    for copy in copies:
+        copy.wait_send()
+
+
+def scatter_scratch(width):
+    return [
+        pltpu.VMEM((2, 4, 4, HALF, width), jnp.bfloat16),
+        pltpu.VMEM((2, 4, 4, HALF, width), jnp.bfloat16),
+        pltpu.VMEM((2, 4, 4, HALF, width), jnp.bfloat16),
+        pltpu.VMEM((2, 2, 2, HALF, width), jnp.bfloat16),
+        pltpu.VMEM((2, 2, 4, HALF, width), jnp.bfloat16),
+        pltpu.VMEM((2, 2, 16, width), jnp.bfloat16),
+        pltpu.VMEM((2, 2, HALF, width), jnp.bfloat16),
+        pltpu.VMEM((2, 3, HALF, width), jnp.bfloat16),
+    ] + [pltpu.SemaphoreType.DMA((n,)) for n in (8, 8, 4, 4, 4, 4, 4, 4, 4, 4)]
+
+
+def scatter_scope(left_ref, right_ref, scratch, finish):
+    width = right_ref.shape[1]
+    depth = right_ref.shape[0]
+    tile = 512
+    other, held, near, early, late, early_two, late_two, total = scratch[:8]
+    flat = scratch[8:]
+    sems = [(flat[2 * i], flat[2 * i + 1]) for i in range(5)]
+
+    def make(dst, add, half, core, big):
+        if half == 0:
+            rows = left_ref[core, big, :, 0:HALF, :]
+        else:
+            rows = left_ref[core, :, big, HALF:ROWS, :]
+        rows = rows.reshape(4 * HALF, depth)
+
+        def column(i, carry):
+            cols = pl.ds(pl.multiple_of(i * tile, tile), tile)
+            value = jnp.dot(rows, right_ref[:, cols], preferred_element_type=jnp.float32)
+            value = value.reshape(4, HALF, tile)
+            if add is not None:
+                value = value + add[:, :, cols].astype(jnp.float32)
+            dst[:, :, cols] = value.astype(jnp.bfloat16)
+            return carry
+
+        lax.fori_loop(0, width // tile, column, 0)
+
+    scatter_steps(
+        make, other, held, near, early, late, early_two, late_two, total, sems, finish
+    )
+
+
+def mix_kernel(left_ref, right_ref, base_ref, gain_ref, res_ref, normed_ref, *scratch):
+    meet()
+
+    def finish(half, value):
+        rows = pl.ds(half * HALF, HALF)
+        value = value + base_ref[rows, :].astype(jnp.float32)
+        res_ref[rows, :] = value
+        scaling = lax.rsqrt(jnp.mean(value * value, axis=-1, keepdims=True) + EPSILON)
+        normed_ref[rows, :] = (value * scaling * gain_ref[...]).astype(jnp.bfloat16)
+
+    scatter_scope(left_ref, right_ref, scratch, finish)
+
+
+def down_kernel(left_ref, right_ref, base_ref, out_ref, *scratch):
+    meet()
+
+    def finish(half, value):
+        rows = pl.ds(half * HALF, HALF)
+        out_ref[rows, :] = (value + base_ref[rows, :]).astype(jnp.bfloat16)
+
+    scatter_scope(left_ref, right_ref, scratch, finish)
+
+
+VM = pl.BlockSpec(memory_space=pltpu.VMEM)
+
+
+def remote_params(number):
+    return pltpu.CompilerParams(
+        collective_id=number, has_side_effects=True, vmem_limit_bytes=60 * 1024 * 1024
+    )
+
+
+def mix(left, right, base, gain):
+    width = right.shape[1]
+    return pl.pallas_call(
+        mix_kernel,
+        in_specs=[VM] * 4,
+        out_specs=[VM] * 2,
+        out_shape=[
+            jax.ShapeDtypeStruct((ROWS, width), jnp.float32),
+            jax.ShapeDtypeStruct((ROWS, width), jnp.bfloat16),
+        ],
+        scratch_shapes=scatter_scratch(width),
+        compiler_params=remote_params(1),
+        name="mix",
+    )(left.reshape(2, 4, 4, ROWS, -1), right, base, gain.reshape(1, width))
+
+
+def down(left, right, base):
+    width = right.shape[1]
+    return pl.pallas_call(
+        down_kernel,
+        in_specs=[VM] * 3,
+        out_specs=VM,
+        out_shape=jax.ShapeDtypeStruct((ROWS, width), jnp.bfloat16),
+        scratch_shapes=scatter_scratch(width),
+        compiler_params=remote_params(2),
+        name="down",
+    )(left.reshape(2, 4, 4, ROWS, -1), right, base)
+
+
+def gather_steps(x_ref, buf, sems, use):
+    core = lax.axis_index("core")
+    axes = ("z", "x")
+    rings = (ring("z"), ring("x"))
+    copies = []
+
+    def go(copy):
+        copy.start()
+        copies.append(copy)
+        return copy
+
+    def spot(half, big, small, c=None):
+        return buf.at[half, big, core if c is None else c, small]
+
+    one = {}
+    cores = {}
+    for half in range(2):
+        big = rings[half][0]
+        me, right, left, _ = rings[1 - half]
+        buf[half, big, core, me] = x_ref[half * HALF : (half + 1) * HALF, :]
+        for side, peer in ((0, right), (1, left)):
+            one[half, side] = go(
+                push(
+                    x_ref.at[pl.ds(half * HALF, HALF)],
+                    spot(half, big, me),
+                    sems[0],
+                    half * 2 + side,
+                    axes[1 - half],
+                    peer,
+                )
+            )
+        cores[half, 0] = go(
+            push(
+                x_ref.at[pl.ds(half * HALF, HALF)],
+                spot(half, big, me),
+                sems[1],
+                half * 4,
+                "core",
+                1 - core,
+            )
+        )
+    two = {}
+    for half in range(2):
+        big = rings[half][0]
+        me, right, left, far = rings[1 - half]
+        for side, (frm, to) in ((0, (left, right)), (1, (right, left))):
+            one[half, side].wait_recv()
+            piece = buf.at[half, big, core, frm, pl.ds(16 * side, 16)]
+            two[half, side] = go(
+                push(piece, piece, sems[2], half * 2 + side, axes[1 - half], to)
+            )
+            whole = spot(half, big, frm)
+            cores[half, 1 + side] = go(
+                push(whole, whole, sems[1], half * 4 + 1 + side, "core", 1 - core)
+            )
+    three = {}
+    for half in range(2):
+        big, right, left, _ = rings[half]
+        far = rings[1 - half][3]
+        for side in range(2):
+            two[half, side].wait_recv()
+        whole = spot(half, big, far)
+        chunk = buf.at[half, big, core]
+        for side, peer in ((0, right), (1, left)):
+            three[half, side] = go(
+                push(chunk, chunk, sems[3], half * 2 + side, axes[half], peer)
+            )
+        cores[half, 3] = go(push(whole, whole, sems[1], half * 4 + 3, "core", 1 - core))
+    for half in range(2):
+        for i in range(4):
+            cores[half, i].wait_recv()
+        use(half, rings[half][0])
+    four = {}
+    fives = {}
+    for half in range(2):
+        big, right, left, far = rings[half]
+        for side, (frm, to) in ((0, (left, right)), (1, (right, left))):
+            three[half, side].wait_recv()
+            piece = buf.at[half, frm, core, pl.ds(2 * side, 2)]
+            four[half, side] = go(push(piece, piece, sems[4], half * 2 + side, axes[half], to))
+            chunk = buf.at[half, frm, core]
+            fives[half, side] = go(
+                push(chunk, chunk, sems[5], half * 4 + side, "core", 1 - core)
+            )
+    for half in range(2):
+        _, right, left, _ = rings[half]
+        for side, frm in ((0, left), (1, right)):
+            fives[half, side].wait_recv()
+            use(half, frm)
+    for half in range(2):
+        far = rings[half][3]
+        for side in range(2):
+            four[half, side].wait_recv()
+            piece = buf.at[half, far, core, pl.ds(2 * side, 2)]
+            fives[half, 2 + side] = go(
+                push(piece, piece, sems[5], half * 4 + 2 + side, "core", 1 - core)
+            )
+    for half in range(2):
+        for side in range(2):
+            fives[half, 2 + side].wait_recv()
+        use(half, rings[half][3])
+    for copy in copies:
+        copy.wait_send()
+
+
+def gather_scratch(width):
+    return [pltpu.VMEM((2, 4, 2, 4, HALF, width), jnp.bfloat16)] + [
+        pltpu.SemaphoreType.DMA((n,)) for n in (4, 4, 8, 8, 4, 4, 4, 4, 4, 4, 8, 8)
+    ]
+
+
+def gather_scope(x_ref, scratch, use):
+    buf = scratch[0]
+    sems = [(scratch[1 + 2 * i], scratch[2 + 2 * i]) for i in range(6)]
+    gather_steps(x_ref, buf, sems, use)
+
+
+def project_kernel(x_ref, w_ref, out_ref, *scratch):
+    meet()
+    buf = scratch[0]
+
+    def use(half, big):
+        rows = buf[half, big].reshape(8 * HALF, x_ref.shape[1])
+        value = jnp.dot(rows, w_ref[...], preferred_element_type=jnp.float32)
+        value = value.reshape(2, 4, HALF, w_ref.shape[1])
+        if half == 0:
+            out_ref[:, big, :, 0:HALF, :] = value
+        else:
+            out_ref[:, :, big, HALF:ROWS, :] = value
+
+    gather_scope(x_ref, scratch, use)
+
+
+def lift_kernel(x_ref, w_ref, out_ref, *scratch):
+    meet()
+    buf = scratch[0]
+    units = out_ref.shape[-1]
+
+    def use(half, big):
+        rows = buf[half, big].reshape(8 * HALF, x_ref.shape[1])
+        value = jnp.dot(rows, w_ref[...], preferred_element_type=jnp.float32)
+        gate, up = value[:, :units], value[:, units:]
+        value = (gate / (1.0 + jnp.exp(-gate)) * up).astype(jnp.bfloat16)
+        value = value.reshape(2, 4, HALF, units)
+        if half == 0:
+            out_ref[:, big, :, 0:HALF, :] = value
+        else:
+            out_ref[:, :, big, HALF:ROWS, :] = value
+
+    gather_scope(x_ref, scratch, use)
+
+
+def project(x, w):
+    n = w.shape[1]
+    return pl.pallas_call(
+        project_kernel,
+        in_specs=[VM] * 2,
+        out_specs=VM,
+        out_shape=jax.ShapeDtypeStruct((2, 4, 4, ROWS, n), jnp.float32),
+        scratch_shapes=gather_scratch(x.shape[1]),
+        compiler_params=remote_params(3),
+        name="project",
+    )(x, w).reshape(32 * ROWS, n)
+
+
+def lift(x, w):
+    units = w.shape[1] // 2
+    return pl.pallas_call(
+        lift_kernel,
+        in_specs=[VM] * 2,
+        out_specs=VM,
+        out_shape=jax.ShapeDtypeStruct((2, 4, 4, ROWS, units), jnp.bfloat16),
+        scratch_shapes=gather_scratch(x.shape[1]),
+        compiler_params=remote_params(4),
+        name="lift",
+    )(x, w).reshape(32 * ROWS, units)
+
+
 def rope_tables(positions):
     inverse = 1.0 / ROPE_BASE ** (jnp.arange(0, HD, 2).astype(jnp.float32) / HD)
     angles = positions.astype(jnp.float32)[:, None] * inverse[None, :]
@@ -229,8 +687,7 @@
     w_out = own(attention_out)
     w_down = own(down_weight)
 
-    normed = lax.all_gather(rms_norm(states, attention_gain), PLANE, axis=0, tiled=True)
-    joined = jnp.dot(normed, w_qkv, preferred_element_type=jnp.float32)
+    joined = project(rms_norm(states, attention_gain), w_qkv)
 
     own_map = lax.dynamic_slice_in_dim(block_map, y_lo * 8, 8)
     at = jnp.arange(256, dtype=jnp.int32)
@@ -271,17 +728,9 @@
     )
     cache = jnp.where(core == y_hi, cache_rows(core), partner)
 
-    def scatter(left, right):
-        partial = jnp.dot(left, right, preferred_element_type=jnp.float32).astype(jnp.bfloat16)
-        return lax.psum_scatter(partial, PLANE, scatter_dimension=0, tiled=True).astype(
-            jnp.float32
-        )
-
-    residual = states.astype(jnp.float32) + scatter(attended, w_out)
-    normed_two = lax.all_gather(rms_norm(residual, forward_gain), PLANE, axis=0, tiled=True)
-    lifted = jnp.dot(normed_two, w_gu, preferred_element_type=jnp.float32)
-    activated = (jax.nn.silu(lifted[:, :units]) * lifted[:, units:]).astype(jnp.bfloat16)
-    hidden_out = (residual + scatter(activated, w_down)).astype(jnp.bfloat16)
+    residual, normed_two = mix(attended, w_out, states, forward_gain)
+    activated = lift(normed_two, w_gu)
+    hidden_out = down(activated, w_down, residual)
     return (hidden_out, cache[0], cache[1])
 
 

time: 580 us -> 507 us (0.87); the launches traced: 579 us -> 498 us
  waiting for transfers between devices: 391 us -> 90.7 us
  Pallas kernels: 30.9 us -> 247 us
  matrix products: 34.4 us -> 0 us
  starting transfers between devices: 23.7 us -> 46.8 us
  other arithmetic: 28.3 us -> 45.6 us
    pallas_call x0 -> x4, Pallas kernels: none -> 212 us  [the longest x1 59.4 us: down(): pl.pallas_call(down_kernel, in_specs=[VM] * 3, out_specs=VM, out_shape=ja...]
    reduce_scatter x2 -> x0, waiting for transfers between devices: 199 us -> none  [scatter(): lax.psum_scatter(partial, PLANE, scatter_dimension=0, tiled=True)]
    ppermute x2, waiting for transfers between devices: 59 us -> 0.01 us  [spread(): other = lax.ppermute(mine, ('y_lo', 'core', 'y_hi'), flip)]
    dot_general x4 -> x0, matrix products: 34.4 us -> none  [the longest x2 17 us: scatter(): jnp.dot(left, right, preferred_element_type=jnp.float32)]
    all_gather x1, waiting for transfers between devices: 59.7 us -> 29.5 us  [body(): kv_all = lax.all_gather(kv, ('y_lo', 'y_hi'), axis=1)]
    ppermute x1, starting transfers between devices: 2.23 us -> 17.2 us  [body(): lax.ppermute(cache_rows(1 - core), ('core', 'y_hi'), [(b * 2 + b, (1 - b)...]
    all_to_all x2, waiting for transfers between devices: 71.6 us -> 61.2 us  [spread(): lax.all_to_all(both, ('z', 'x'), split_axis=0, concat_axis=0, tiled=True)]
    ppermute x2, starting transfers between devices: 3.45 us -> 12.2 us  [spread(): other = lax.ppermute(mine, ('y_lo', 'core', 'y_hi'), flip)]
  transfers between devices with their start and end apart: 12 -> 8, of which waited for: 8 -> 3; matrix products, arithmetic and copies ran while one was open for 14% -> 16% of each run, Pallas kernels for 5% -> 50%
where the time goes in v2:
time: 507 us; the launch traced here: 498 us
  Pallas kernels  247 us (49%)
  waiting for transfers between devices  90.7 us (18%)
  local copies, waits for them, and re-layouts  53.5 us (11%)
  starting transfers between devices  46.8 us (9%)
  other arithmetic  45.6 us (9%)
  between operations  14.5 us (3%)
    all_to_all x2, waiting for transfers between devices, spread(): lax.all_to_all(both, ('z', 'x'), split_axis=0, concat_axis=0, tiled=True)  61.2 us
    pallas_call x1, Pallas kernels, down(): pl.pallas_call(down_kernel, in_specs=[VM] * 3, out_specs=VM, out_shape=ja...  59.4 us
    pallas_call x1, Pallas kernels, mix(): pl.pallas_call(mix_kernel, in_specs=[VM] * 4, out_specs=[VM] * 2, out_sha...  56.2 us
    pallas_call x1, Pallas kernels, lift(): pl.pallas_call(lift_kernel, in_specs=[VM] * 2, out_specs=VM, out_shape=ja...  49 us
    pallas_call x1, Pallas kernels, project(): pl.pallas_call(project_kernel, in_specs=[VM] * 2, out_specs=VM, out_shape...  47.5 us
    pallas_call x1, Pallas kernels, attention(): pl.pallas_call(attention_kernel, grid_spec=pltpu.PrefetchScalarGridSpec(n...  34.7 us
    all_gather x1, waiting for transfers between devices, body(): kv_all = lax.all_gather(kv, ('y_lo', 'y_hi'), axis=1)  29.5 us
    ppermute x1, starting transfers between devices, body(): lax.ppermute(cache_rows(1 - core), ('core', 'y_hi'), [(b * 2 + b, (1 - b)...  17.2 us
  transfers between devices with their start and end apart: 8, of which 3 were waited for; matrix products, arithmetic and copies ran while one was open for 16% of the time, Pallas kernels for 50%

profile of v2, /device:TPU:14, one launch (start us, length us, event | category | flops | bytes accessed | tf_op | source)
XLA Modules:
  0.0 497.9 jit_solution(15304433042784119532)
XLA Ops:
  7.2 3.5 convert_element_type.58
  10.6 3.7 reshape.316
  14.3 2.4 constant_dynamic-slice_fusion.3
  16.7 1.4 copy-done
  18.2 1.3 copy.86
  19.4 1.6 collective-permute-start
  21.0 3.1 convert_element_type.64
  24.1 4.0 reshape.320
  28.1 5.8 %constant_dynamic-slice_fusion.2 = bf16[96,2,16,1,256]{4,3,2,1,0:T(2,128)(2,1)S(1)} fusion(bf16[96,2,16,2,256]{4,3,2,1,0:T(2,128)(2,1)} %reshape.320, s32[]{:T(128)S(6)} %select_n.178), kind=kLoop, calls=%fused_computation.75 | loop fusion | bytes 3145732 | tf_op jit(solution)/shard_map/jit(dynamic_index_in_dim)/dynamic_slice | solution.py:671
  33.9 3.6 copy.85
  37.5 10.6 %collective-permute-start.2 = (bf16[96,2,16,256]{3,1,0,2:T(2,128)(2,1)}, bf16[96,2,16,256]{3,1,0,2:T(2,128)(2,1)}, u32[]{:S(2)}, u32[]{:S(2)}) collective-permute-start(bf16[96,2,16,256]{3,1,0,2:T(2,128)(2,1)} %bitcast.58), channel_id=1, source_target_pairs={{0,65},{1,64},{32,97},{33,96},{64,1},{65,0},{96,33},{97,32},{2,67}... | collective-permute-start | bytes 4718600 | tf_op jit(solution)/shard_map/ppermute | solution.py:672
  49.2 2.2 select_bitcast_fusion.1
  52.0 2.1 copy.61
  54.1 8.4 %all-to-all-start = ((bf16[16,2,96,3,96]{4,2,3,1,0:T(8,128)(2,1)}), bf16[16,2,96,3,96]{4,2,3,1,0:T(8,128)(2,1)}, u32[]{:S(2)}, u32[]{:S(2)}) async-start(bf16[16,2,96,3,96]{4,2,3,1,0:T(8,128)(2,1)} %copy.61), calls=%async_computation | async-start | bytes 4718592 | tf_op jit(solution)/shard_map/all_to_all | solution.py:677
  63.2 0.7 convert_bitcast_fusion
  64.7 1.6 fusion.20.x_ref
  66.3 26.8 %all-to-all-done = bf16[16,2,96,3,96]{4,2,3,1,0:T(8,128)(2,1)} async-done(((bf16[16,2,96,3,96]{4,2,3,1,0:T(8,128)(2,1)}), bf16[16,2,96,3,96]{4,2,3,1,0:T(8,128)(2,1)}, u32[]{:S(2)}, u32[]{:S(2)}) %all-to-all-start) | async-done | bytes 1769504 | tf_op jit(solution)/shard_map/all_to_all | solution.py:677
  93.1 5.0 copy.72
  98.1 7.2 %reshape.330.w_ref = bf16[3072,288]{1,0:T(8,128)(2,1)} reshape(bf16[16,2,96,3,96]{4,3,2,1,0:T(4,128)(2,1)} %copy.72) | data formatting | bytes 3538944 | tf_op jit(solution)/shard_map/reshape | solution.py:678
  105.3 47.5 %project.1 = f32[2,4,4,64,288]{4,3,2,1,0:T(8,128)} custom-call(bf16[64,3072]{1,0:T(8,128)(2,1)} %fusion.20.x_ref, bf16[3072,288]{1,0:T(8,128)(2,1)} %reshape.330.w_ref), custom_call_target="tpu_custom_call" | custom-call | tf_op jit(solution)/shard_map/project/pallas_call | solution.py:595
  152.8 1.8 fusion.21
  154.7 8.5 %fusion.23 = (bf16[1,2048,48]{2,1,0:T(8,128)(2,1)S(1)}, bf16[1,2048,48]{2,1,0:T(8,128)(2,1)S(1)}, bf16[2048,48]{1,0:T(8,128)(2,1)}, bf16[2048,48]{1,0:T(8,128)(2,1)}) fusion(f32[2048,288]{1,0:T(8,128)} %bitcast.61, f32[48]{0:T(128)S(1)} %copy-done.8, f32[2048]{0:T(1024)S(1)} %bitcast.71), kind=kLoop, calls=%fused_computation.45 | loop fusion | flops 1671168 | bytes 2367680 | tf_op jit(solution)/shard_map/concatenate | solution.py:628
  163.2 1.4 pad_maximum_fusion
  164.6 5.0 %fusion = (bf16[1,96,2,16,256]{4,2,1,0,3:T(2,128)(2,1)S(1)}, bf16[1,96,2,16,256]{4,2,1,0,3:T(2,128)(2,1)S(1)}) fusion(bf16[96,2,16,256]{3,1,0,2:T(2,128)(2,1)} %collective-permute-done.2, pred[]{:T(512)S(6)} %eq.47, bf16[96,2,16,1,256]{4,3,2,1,0:T(2,128)(2,1)S(1)} %constant_dynamic-slice_fusion.2), kind=kLoop, calls=%fused_computation.4 | loop fusion | flops 1572864 | bytes 6291457 | tf_op jit(solution)/shard_map/stack | solution.py:675
  169.6 6.1 %maximum_bitcast_fusion = bf16[16,2,96,2,256]{4,3,2,1,0:T(2,128)(2,1)} fusion(bf16[1,96,2,16,256]{4,2,1,0,3:T(2,128)(2,1)S(1)} %get-tuple-element.33, bf16[1,96,2,16,256]{4,2,1,0,3:T(2,128)(2,1)S(1)} %get-tuple-element.32), kind=kLoop, calls=%fused_computation | loop fusion | flops 1572864 | bytes 6291456 | tf_op jit(solution)/shard_map/transpose | solution.py:676
  175.6 5.5 %all-to-all-start.1 = ((bf16[16,2,96,2,256]{4,3,2,1,0:T(2,128)(2,1)}), bf16[16,2,96,2,256]{4,3,2,1,0:T(2,128)(2,1)}, u32[]{:S(2)}, u32[]{:S(2)}) async-start(bf16[16,2,96,2,256]{4,3,2,1,0:T(2,128)(2,1)} %maximum_bitcast_fusion), calls=%async_computation.1 | async-start | bytes 6291456 | tf_op jit(solution)/shard_map/all_to_all | solution.py:677
  181.1 2.2 convert_element_type.63
  183.3 1.7 collective-permute-start.1
  184.9 1.4 convert_element_type.65
  186.3 1.8 collective-permute-start.3
  188.2 0.6 select_reduce_fusion.1.slot_of
  190.2 2.2 broadcast_select_fusion.4.right_ref
  192.4 1.4 broadcast_select_fusion.2.right_ref
  193.8 1.1 pad_maximum_fusion.1.q_ref
  194.9 34.4 %all-to-all-done.1 = bf16[16,2,96,2,256]{4,3,2,1,0:T(2,128)(2,1)} async-done(((bf16[16,2,96,2,256]{4,3,2,1,0:T(2,128)(2,1)}), bf16[16,2,96,2,256]{4,3,2,1,0:T(2,128)(2,1)}, u32[]{:S(2)}, u32[]{:S(2)}) %all-to-all-start.1) | async-done | bytes 3145760 | tf_op jit(solution)/shard_map/all_to_all | solution.py:677
  229.4 4.1 copy.78
  233.5 29.5 %all-gather.3.cloned.1.call-done = bf16[2,8192,96]{2,1,0:T(8,128)(2,1)} async-done(((bf16[2,2048,96]{2,1,0:T(8,128)(2,1)}), bf16[2,8192,96]{2,1,0:T(8,128)(2,1)}) %all-gather.3.cloned.1.call-update) | async-done | bytes 3145744 | tf_op jit(solution)/shard_map/all_gather | solution.py:704
  262.9 1.7 constant_dynamic-slice_fusion
  265.3 17.2 %collective-permute-start.4 = (bf16[2,2048,96]{1,2,0:T(8,128)(2,1)S(1)}, bf16[2,2048,96]{1,2,0:T(8,128)(2,1)}, u32[]{:S(2)}, u32[]{:S(2)}) collective-permute-start(bf16[2,2048,96]{1,2,0:T(8,128)(2,1)S(1)} %copy.68), channel_id=1, source_target_pairs={{0,32},{33,1},{2,34},{35,3},{4,36},{37,5},{6,38},{39,7},{8,40},{41... | collective-permute-start | bytes 2359304 | tf_op jit(solution)/shard_map/ppermute | solution.py:724
  282.5 4.4 fusion.30
  287.1 34.7 %attention.1 = bf16[8,256,96]{2,1,0:T(8,128)(2,1)} custom-call(s32[8]{0:T(128)} %copy-done.11, s32[16]{0:T(128)} %select_reduce_fusion.1.slot_of, s32[2]{0:T(128)} %pad_add_fusion.1.half_ref, bf16[8,256,96]{2,1,0:T(8,128)(2,1)} %pad_maximum_fusion.1.q_ref, bf16[32,256,96]{2,1,0:T(8,128)(2,1)} %bitcast.69, bf16[32,256,96]{2,1,0:T(8,128)(2,1)} %bitcast.68, ...), custom_call_target="tpu_custom_call" | custom-call | flops 8000000000 | bytes 8000000 | tf_op jit(solution)/shard_map/attention/pallas_call | solution.py:135
  321.8 56.2 %mix.1 = (f32[64,3072]{1,0:T(8,128)}, bf16[64,3072]{1,0:T(8,128)(2,1)}) custom-call(bf16[2,4,4,64,96]{4,3,2,1,0:T(8,128)(2,1)} %bitcast.70, bf16[96,3072]{1,0:T(8,128)(2,1)} %broadcast_select_fusion.4.right_ref, bf16[64,3072]{1,0:T(8,128)(2,1)} %base_ref.1, f32[1,3072]{1,0:T(1,128)} %bitcast.72), custom_call_target="tpu_custom_call" | custom-call | tf_op jit(solution)/shard_map/mix/pallas_call | solution.py:414
  378.0 49.0 %lift.1.left_ref = bf16[2,4,4,64,256]{4,3,2,1,0:T(8,128)(2,1)} custom-call(bf16[64,3072]{1,0:T(8,128)(2,1)} %get-tuple-element.5.x_ref, bf16[3072,512]{1,0:T(8,128)(2,1)} %bitcast.62), custom_call_target="tpu_custom_call" | custom-call | tf_op jit(solution)/shard_map/lift/pallas_call | solution.py:608
  427.0 59.4 %down.1 = bf16[64,3072]{1,0:T(8,128)(2,1)} custom-call(bf16[2,4,4,64,256]{4,3,2,1,0:T(8,128)(2,1)} %lift.1.left_ref, bf16[256,3072]{1,0:T(8,128)(2,1)} %broadcast_select_fusion.2.right_ref, f32[64,3072]{1,0:T(8,128)} %get-tuple-element.6.base_ref), custom_call_target="tpu_custom_call" | custom-call | tf_op jit(solution)/shard_map/down/pallas_call | solution.py:430
  486.4 1.6 copy.69
  488.2 1.0 copy.70
  489.2 1.0 copy.71
  490.1 0.7 copy.88
  (50 shorter events, 5.4 us)
Async XLA Ops:
  16.7 1.4 copy-start
  19.4 29.8 %collective-permute-start = (bf16[96,3,16,96]{3,2,1,0:T(8,128)(2,1)}, bf16[96,3,16,96]{3,2,1,0:T(8,128)(2,1)}, u32[]{:S(2)}, u32[]{:S(2)}) collective-permute-start(bf16[96,3,16,96]{3,2,1,0:T(8,128)(2,1)} %bitcast.59), channel_id=1, source_target_pairs={{0,65},{1,64},{32,97},{33,96},{64,1},{65,0},{96,33},{97,32},{2,67}... | collective-permute-start | bytes 2654216 | tf_op jit(solution)/shard_map/ppermute | solution.py:672
  33.9 14.2 %copy-start.9 = (s32[16]{0:T(128)S(1)}, s32[16]{0:T(128)}, u32[]{:S(2)}) copy-start(s32[16]{0:T(128)} %param.16) | copy-start | bytes 196
  37.5 127.1 %collective-permute-start.2 = (bf16[96,2,16,256]{3,1,0,2:T(2,128)(2,1)}, bf16[96,2,16,256]{3,1,0,2:T(2,128)(2,1)}, u32[]{:S(2)}, u32[]{:S(2)}) collective-permute-start(bf16[96,2,16,256]{3,1,0,2:T(2,128)(2,1)} %bitcast.58), channel_id=1, source_target_pairs={{0,65},{1,64},{32,97},{33,96},{64,1},{65,0},{96,33},{97,32},{2,67}... | collective-permute-start | bytes 4718600 | tf_op jit(solution)/shard_map/ppermute | solution.py:672
  48.7 2.8 copy-start.11
  54.1 10.4 %copy-start.2 = (bf16[64,3072]{1,0:T(8,128)(2,1)S(1)}, bf16[64,3072]{1,0:T(8,128)(2,1)}, u32[]{:S(2)}) copy-start(bf16[64,3072]{1,0:T(8,128)(2,1)} %base_ref.1) | copy-start | bytes 1179652
  54.1 39.0 %all-to-all-start = ((bf16[16,2,96,3,96]{4,2,3,1,0:T(8,128)(2,1)}), bf16[16,2,96,3,96]{4,2,3,1,0:T(8,128)(2,1)}, u32[]{:S(2)}, u32[]{:S(2)}) async-start(bf16[16,2,96,3,96]{4,2,3,1,0:T(8,128)(2,1)} %copy.61), calls=%async_computation | async-start | bytes 4718592 | tf_op jit(solution)/shard_map/all_to_all | solution.py:677
  62.5 200.4 %all-gather.3.cloned.1.call-start = ((), (), s32[]{:S(2)}) async-start(), calls=%async_computation.2 | async-start | bytes 5242880 | tf_op jit(solution)/shard_map/all_gather | solution.py:704
  105.3 49.3 %copy-start.8 = (f32[48]{0:T(128)S(1)}, f32[48]{0:T(128)}, u32[]{:S(2)}) copy-start(f32[48]{0:T(128)} %negate_power_fusion) | copy-start | bytes 580
  175.6 9.3 %copy-start.1 = (f32[256,3072]{1,0:T(8,128)S(1)}, f32[256,3072]{1,0:T(8,128)}, u32[]{:S(2)}) copy-start(f32[256,3072]{1,0:T(8,128)} %param.15) | copy-start | bytes 9437188
  175.6 53.7 %all-to-all-start.1 = ((bf16[16,2,96,2,256]{4,3,2,1,0:T(2,128)(2,1)}), bf16[16,2,96,2,256]{4,3,2,1,0:T(2,128)(2,1)}, u32[]{:S(2)}, u32[]{:S(2)}) async-start(bf16[16,2,96,2,256]{4,3,2,1,0:T(2,128)(2,1)} %maximum_bitcast_fusion), calls=%async_computation.1 | async-start | bytes 6291456 | tf_op jit(solution)/shard_map/all_to_all | solution.py:677
  183.3 4.9 copy-start.10
  183.3 6.1 %copy-start.6 = (s32[8]{0:T(128)S(1)}, s32[8]{0:T(128)}, u32[]{:S(2)}) copy-start(s32[8]{0:T(128)} %get-tuple-element.22) | copy-start | bytes 100
  183.3 6.2 %copy-start.7 = (s32[32]{0:T(128)S(1)}, s32[32]{0:T(128)}, u32[]{:S(2)}) copy-start(s32[32]{0:T(128)} %param.17) | copy-start | bytes 388
  183.3 6.9 %collective-permute-start.1 = (bf16[96,3072]{1,0:T(8,128)(2,1)}, bf16[96,3072]{1,0:T(8,128)(2,1)}, u32[]{:S(2)}, u32[]{:S(2)}) collective-permute-start(bf16[96,3072]{1,0:T(8,128)(2,1)} %convert_element_type.63), channel_id=1, source_target_pairs={{1,96},{32,65},{65,32},{96,1},{3,98},{34,67},{67,34},{98,3},{5,100... | collective-permute-start | bytes 1769480 | tf_op jit(solution)/shard_map/ppermute | solution.py:682
  186.3 6.1 %collective-permute-start.3 = (bf16[256,3072]{1,0:T(8,128)(2,1)}, bf16[256,3072]{1,0:T(8,128)(2,1)}, u32[]{:S(2)}, u32[]{:S(2)}) collective-permute-start(bf16[256,3072]{1,0:T(8,128)(2,1)} %convert_element_type.65), channel_id=1, source_target_pairs={{1,96},{32,65},{65,32},{96,1},{3,98},{34,67},{67,34},{98,3},{5,100... | collective-permute-start | bytes 4718600 | tf_op jit(solution)/shard_map/ppermute | solution.py:682
  192.4 1.4 copy-start.3
  192.4 1.4 copy-start.4
  265.3 221.2 %collective-permute-start.4 = (bf16[2,2048,96]{1,2,0:T(8,128)(2,1)S(1)}, bf16[2,2048,96]{1,2,0:T(8,128)(2,1)}, u32[]{:S(2)}, u32[]{:S(2)}) collective-permute-start(bf16[2,2048,96]{1,2,0:T(8,128)(2,1)S(1)} %copy.68), channel_id=1, source_target_pairs={{0,32},{33,1},{2,34},{35,3},{4,36},{37,5},{6,38},{39,7},{8,40},{41... | collective-permute-start | bytes 2359304 | tf_op jit(solution)/shard_map/ppermute | solution.py:724
  488.1 2.0 copy-start.5
Sparse Core Ops, SparseCore 0:
  164.7 98.2 all-gather.2

commit v3 on v2

--- a/solution.py
+++ b/solution.py
@@ -36,7 +36,7 @@
 
 
 def attention_kernel(
-    own_map, slot_of, half_ref, q_ref, k_ref, v_ref, live_ref, o_ref, m_ref, l_ref, acc_ref
+    own_map, slot_of, half_ref, q_ref, kv_ref, live_ref, o_ref, m_ref, l_ref, acc_ref
 ):
     step = pl.program_id(0)
     logical = own_map[step]
@@ -55,8 +55,8 @@
     def pair(slot):
         low = slot // 8
         inner = slot % 8
-        keys = jnp.concatenate([k_ref[low * 16 + inner], k_ref[low * 16 + 8 + inner]], axis=0)
-        values = jnp.concatenate([v_ref[low * 16 + inner], v_ref[low * 16 + 8 + inner]], axis=0)
+        keys = jnp.concatenate([kv_ref[low, 0, inner], kv_ref[low + 2, 0, inner]], axis=0)
+        values = jnp.concatenate([kv_ref[low, 1, inner], kv_ref[low + 2, 1, inner]], axis=0)
         return keys, values
 
     def scores_of(keys):
@@ -121,16 +121,15 @@
         @pl.when(logical > span)
         def _():
             slot = slot_of[0]
-            at = (slot // 8) * 16 + slot % 8
-            keys = k_ref[at, 0:128]
-            values = v_ref[at, 0:128]
+            keys = kv_ref[slot // 8, 0, slot % 8, 0:128]
+            values = kv_ref[slot // 8, 1, slot % 8, 0:128]
             allowed = lax.broadcasted_iota(jnp.int32, (rows, 128), 1) < SINKS
             more(jnp.where(allowed, scores_of(keys), MASK_FLOOR), values)
 
     o_ref[0] = (acc_ref[...] / l_ref[...]).astype(jnp.bfloat16)
 
 
-def attention(q, k_all, v_all, own_map, slot_of, places, live):
+def attention(q, kv, own_map, slot_of, places, live):
     slots, rows, _ = q.shape
     return pl.pallas_call(
         attention_kernel,
@@ -139,8 +138,7 @@
             grid=(slots,),
             in_specs=[
                 pl.BlockSpec((1, rows, HD), lambda i, *_: (i, 0, 0)),
-                pl.BlockSpec(k_all.shape, lambda i, *_: (0, 0, 0)),
-                pl.BlockSpec(v_all.shape, lambda i, *_: (0, 0, 0)),
+                pl.BlockSpec(kv.shape, lambda i, *_: (0, 0, 0, 0, 0)),
                 pl.BlockSpec((1, 1, 2 * rows), lambda i, *_: (i, 0, 0)),
             ],
             out_specs=pl.BlockSpec((1, rows, HD), lambda i, *_: (i, 0, 0)),
@@ -155,7 +153,7 @@
             flops=8_000_000_000, bytes_accessed=8_000_000, transcendentals=8_000_000
         ),
         name="attention",
-    )(own_map, slot_of, places, q, k_all, v_all, live)
+    )(own_map, slot_of, places, q, kv, live)
 
 
 MESH = pl.DeviceIdType.MESH
@@ -167,32 +165,116 @@
     return me, lax.rem(me + 1, 4), lax.rem(me + 3, 4), lax.rem(me + 2, 4)
 
 
-def meet():
+def ring_y():
+    me = lax.axis_index("y_hi") * 2 + lax.axis_index("y_lo")
+    return me, lax.rem(me + 1, 4), lax.rem(me + 3, 4), lax.rem(me + 2, 4)
+
+
+def at_y(y):
+    return {"y_hi": lax.div(y, 2), "y_lo": lax.rem(y, 2)}
+
+
+def at_offset(offset):
+    z, x = lax.axis_index("z"), lax.axis_index("x")
+    return {"z": lax.rem(z + offset // 4, 4), "x": lax.rem(x + offset % 4, 4)}
+
+
+def meet(whole=False):
     barrier = pltpu.get_barrier_semaphore()
-    for axis in ("x", "z"):
-        _, right, left, _ = ring(axis)
-        for peer in (right, left):
-            pl.semaphore_signal(barrier, inc=1, device_id={axis: peer}, device_id_type=MESH)
-    pl.semaphore_signal(
-        barrier, inc=1, device_id={"core": 1 - lax.axis_index("core")}, device_id_type=MESH
-    )
-    pl.semaphore_wait(barrier, 5)
+    peers = [{"core": 1 - lax.axis_index("core")}]
+    if whole:
+        peers += [at_offset(offset) for offset in range(1, 16)]
+        peers += [at_y(y) for y in ring_y()[1:3]]
+    else:
+        for axis in ("x", "z"):
+            peers += [{axis: peer} for peer in ring(axis)[1:3]]
+    for peer in peers:
+        pl.semaphore_signal(barrier, inc=1, device_id=peer, device_id_type=MESH)
+    pl.semaphore_wait(barrier, len(peers))
 
 
 def push(src, dst, sems, at, axis, peer):
     send, recv = sems
+    place = peer if axis is None else {axis: peer}
     return pltpu.make_async_remote_copy(
         src_ref=src,
         dst_ref=dst,
         send_sem=send.at[at],
         recv_sem=recv.at[at],
-        device_id={axis: peer},
+        device_id=place,
         device_id_type=MESH,
     )
 
 
+class Spread:
+    def __init__(self, parts, full, sems):
+        self.parts, self.full, self.sems = parts, full, sems
+        self.copies = []
+
+    def go(self, copy):
+        copy.start()
+        self.copies.append(copy)
+        return copy
+
+    def send(self):
+        me = lax.axis_index("z") * 4 + lax.axis_index("x")
+        y = ring_y()[0]
+        self.full[me, y] = self.parts[me]
+        self.one = []
+        for offset in range(1, 16):
+            place = at_offset(offset)
+            self.one.append(
+                self.go(
+                    push(
+                        self.parts.at[place["z"] * 4 + place["x"]],
+                        self.full.at[me, y],
+                        self.sems[0],
+                        offset,
+                        None,
+                        place,
+                    )
+                )
+            )
+
+    def along(self):
+        for copy in self.one:
+            copy.wait_recv()
+        me, right, left, _ = ring_y()
+        piece = self.full.at[:, me]
+        self.two = [
+            self.go(push(piece, piece, self.sems[1], side, None, at_y(peer)))
+            for side, peer in ((0, right), (1, left))
+        ]
+
+    def relay(self):
+        _, right, left, _ = ring_y()
+        self.three = []
+        for side, (frm, to) in ((0, (left, right)), (1, (right, left))):
+            self.two[side].wait_recv()
+            piece = self.full.at[pl.ds(8 * side, 8), frm]
+            self.three.append(
+                self.go(push(piece, piece, self.sems[2], side, None, at_y(to)))
+            )
+
+    def arrive(self):
+        for copy in self.three:
+            copy.wait_recv()
+
+    def done(self):
+        for copy in self.copies:
+            copy.wait_send()
+
+
+def spread_sems():
+    return [pltpu.SemaphoreType.DMA((n,)) for n in (16, 16, 2, 2, 2, 2)]
+
+
+def paired(flat):
+    return [(flat[2 * i], flat[2 * i + 1]) for i in range(len(flat) // 2)]
+
+
 def scatter_steps(
-    make, other, held, near, early, late, early_two, late_two, total, sems, finish
+    make, other, held, near, early, late, early_two, late_two, total, sems, finish, hook
 ):
     core = lax.axis_index("core")
     rings = (ring("z"), ring("x"))
@@ -224,6 +306,7 @@
                 )
             )
 
+    hook(0)
     first = {}
     second = {}
     for half in range(2):
@@ -262,6 +345,7 @@
                     (right, left)[side],
                 )
             )
+    hook(1)
     for half in range(2):
         swaps[half, 3].wait_recv()
         make(held.at[half, 3], near.at[half, 3], half, core, big_at(half, 3))
@@ -346,7 +430,7 @@
     ] + [pltpu.SemaphoreType.DMA((n,)) for n in (8, 8, 4, 4, 4, 4, 4, 4, 4, 4)]
 
 
-def scatter_scope(left_ref, right_ref, scratch, finish):
+def scatter_scope(left_ref, right_ref, scratch, finish, hook=lambda at: None):
     width = right_ref.shape[1]
     depth = right_ref.shape[0]
     tile = 512
@@ -373,12 +457,22 @@
         lax.fori_loop(0, width // tile, column, 0)
 
     scatter_steps(
-        make, other, held, near, early, late, early_two, late_two, total, sems, finish
+        make, other, held, near, early, late, early_two, late_two, total, sems, finish, hook
     )
 
 
-def mix_kernel(left_ref, right_ref, base_ref, gain_ref, res_ref, normed_ref, *scratch):
-    meet()
+def mix_kernel(
+    left_ref, right_ref, base_ref, gain_ref, part_ref, res_ref, normed_ref, full_ref, *scratch
+):
+    meet(True)
+    spread = Spread(part_ref, full_ref, paired(scratch[18:]))
+    spread.send()
+
+    def hook(at):
+        if at == 0:
+            spread.along()
+        else:
+            spread.relay()
 
     def finish(half, value):
         rows = pl.ds(half * HALF, HALF)
@@ -387,7 +481,9 @@
         scaling = lax.rsqrt(jnp.mean(value * value, axis=-1, keepdims=True) + EPSILON)
         normed_ref[rows, :] = (value * scaling * gain_ref[...]).astype(jnp.bfloat16)
 
-    scatter_scope(left_ref, right_ref, scratch, finish)
+    scatter_scope(left_ref, right_ref, scratch[:18], finish, hook)
+    spread.arrive()
+    spread.done()
 
 
 def down_kernel(left_ref, right_ref, base_ref, out_ref, *scratch):
@@ -409,20 +505,21 @@
     )
 
 
-def mix(left, right, base, gain):
+def mix(left, right, base, gain, parts):
     width = right.shape[1]
     return pl.pallas_call(
         mix_kernel,
-        in_specs=[VM] * 4,
-        out_specs=[VM] * 2,
+        in_specs=[VM] * 5,
+        out_specs=[VM] * 3,
         out_shape=[
             jax.ShapeDtypeStruct((ROWS, width), jnp.float32),
             jax.ShapeDtypeStruct((ROWS, width), jnp.bfloat16),
+            jax.ShapeDtypeStruct((16, 4) + parts.shape[1:], jnp.bfloat16),
         ],
-        scratch_shapes=scatter_scratch(width),
+        scratch_shapes=scatter_scratch(width) + spread_sems(),
         compiler_params=remote_params(1),
         name="mix",
-    )(left.reshape(2, 4, 4, ROWS, -1), right, base, gain.reshape(1, width))
+    )(left.reshape(2, 4, 4, ROWS, -1), right, base, gain.reshape(1, width), parts)
 
 
 def down(left, right, base):
@@ -438,7 +535,7 @@
     )(left.reshape(2, 4, 4, ROWS, -1), right, base)
 
 
-def gather_steps(x_ref, buf, sems, use):
+def gather_steps(x_ref, buf, sems, use, hook):
     core = lax.axis_index("core")
     axes = ("z", "x")
     rings = (ring("z"), ring("x"))
@@ -479,6 +576,7 @@
                 1 - core,
             )
         )
+    hook(0)
     two = {}
     for half in range(2):
         big = rings[half][0]
@@ -493,6 +591,7 @@
             cores[half, 1 + side] = go(
                 push(whole, whole, sems[1], half * 4 + 1 + side, "core", 1 - core)
             )
+    hook(1)
     three = {}
     for half in range(2):
         big, right, left, _ = rings[half]
@@ -506,6 +605,7 @@
                 push(chunk, chunk, sems[3], half * 2 + side, axes[half], peer)
             )
         cores[half, 3] = go(push(whole, whole, sems[1], half * 4 + 3, "core", 1 - core))
+    hook(2)
     for half in range(2):
         for i in range(4):
             cores[half, i].wait_recv()
@@ -549,26 +649,87 @@
     ]
 
 
-def gather_scope(x_ref, scratch, use):
+def gather_scope(x_ref, scratch, use, hook=lambda at: None):
     buf = scratch[0]
     sems = [(scratch[1 + 2 * i], scratch[2 + 2 * i]) for i in range(6)]
-    gather_steps(x_ref, buf, sems, use)
-
-
-def project_kernel(x_ref, w_ref, out_ref, *scratch):
-    meet()
+    gather_steps(x_ref, buf, sems, use, hook)
+
+
+def project_kernel(x_ref, part_ref, cos_ref, sin_ref, q_ref, kv_ref, full_ref, *scratch):
+    meet(True)
     buf = scratch[0]
+    spread = Spread(part_ref, full_ref, paired(scratch[13:19]))
+    sems = paired(scratch[19:23])
+    y, right, left, far = ring_y()
+    width = x_ref.shape[1]
+    started, passed, copies = [], [], []
+
+    def hook(at):
+        if at == 0:
+            spread.send()
+        elif at == 1:
+            spread.along()
+        else:
+            spread.relay()
+            spread.arrive()
+
+    def window(half, big):
+        if half == 0:
+            return (slice(None), big, slice(None), pl.ds(0, HALF), slice(None))
+        return (slice(None), slice(None), big, pl.ds(HALF, HALF), slice(None))
+
+    def flip(value):
+        return jnp.concatenate([value[:, HD // 2 :], value[:, : HD // 2]], axis=1)
+
+    def forward(limit):
+        while len(passed) < limit:
+            index = len(passed)
+            half, big, pushes = started[index]
+            now = []
+            for side, (frm, to) in ((0, (left, right)), (1, (right, left))):
+                pushes[side].wait_recv()
+                piece = kv_ref.at[(frm, side) + window(half, big)]
+                copy = push(piece, piece, sems[1], index * 2 + side, None, at_y(to))
+                copy.start()
+                copies.append(copy)
+                now.append(copy)
+            passed.append(now)
 
     def use(half, big):
-        rows = buf[half, big].reshape(8 * HALF, x_ref.shape[1])
-        value = jnp.dot(rows, w_ref[...], preferred_element_type=jnp.float32)
-        value = value.reshape(2, 4, HALF, w_ref.shape[1])
-        if half == 0:
-            out_ref[:, big, :, 0:HALF, :] = value
-        else:
-            out_ref[:, :, big, HALF:ROWS, :] = value
-
-    gather_scope(x_ref, scratch, use)
+        rows = buf[half, big].reshape(8 * HALF, width)
+        value = jnp.dot(
+            rows, full_ref[...].reshape(width, 3 * 128), preferred_element_type=jnp.float32
+        )
+        at = window(half, big)
+        cosine = cos_ref[at].reshape(8 * HALF, HD)
+        sine = sin_ref[at].reshape(8 * HALF, HD)
+        shape = (2, 4, HALF, HD)
+        query = value[:, 0:HD]
+        key = value[:, 128 : 128 + HD]
+        q_ref[at] = (query * cosine + flip(query) * sine).astype(jnp.bfloat16).reshape(shape)
+        kv_ref[(y, 0) + at] = (
+            (key * cosine + flip(key) * sine).astype(jnp.bfloat16).reshape(shape)
+        )
+        kv_ref[(y, 1) + at] = value[:, 256 : 256 + HD].astype(jnp.bfloat16).reshape(shape)
+        index = len(started)
+        pushes = []
+        for side, peer in ((0, right), (1, left)):
+            piece = kv_ref.at[(y, slice(None)) + at]
+            copy = push(piece, piece, sems[0], index * 2 + side, None, at_y(peer))
+            copy.start()
+            copies.append(copy)
+            pushes.append(copy)
+        started.append((half, big, pushes))
+        forward(index)
+
+    gather_scope(x_ref, scratch[:13], use, hook)
+    forward(8)
+    for now in passed:
+        for copy in now:
+            copy.wait_recv()
+    for copy in copies:
+        copy.wait_send()
+    spread.done()
 
 
 def lift_kernel(x_ref, w_ref, out_ref, *scratch):
@@ -590,17 +751,23 @@
     gather_scope(x_ref, scratch, use)
 
 
-def project(x, w):
-    n = w.shape[1]
+def project(x, parts, cosine, sine):
+    shape = (2, 4, 4, ROWS, HD)
     return pl.pallas_call(
         project_kernel,
-        in_specs=[VM] * 2,
-        out_specs=VM,
-        out_shape=jax.ShapeDtypeStruct((2, 4, 4, ROWS, n), jnp.float32),
-        scratch_shapes=gather_scratch(x.shape[1]),
+        in_specs=[VM] * 4,
+        out_specs=[VM] * 2,
+        out_shape=[
+            jax.ShapeDtypeStruct(shape, jnp.bfloat16),
+            jax.ShapeDtypeStruct((4, 2) + shape, jnp.bfloat16),
+        ],
+        scratch_shapes=[pltpu.VMEM((16, 4) + parts.shape[1:], jnp.bfloat16)]
+        + gather_scratch(x.shape[1])
+        + spread_sems()
+        + [pltpu.SemaphoreType.DMA((16,)) for _ in range(4)],
         compiler_params=remote_params(3),
         name="project",
-    )(x, w).reshape(32 * ROWS, n)
+    )(x, parts, cosine.reshape(shape), sine.reshape(shape))
 
 
 def lift(x, w):
@@ -619,15 +786,11 @@
 def rope_tables(positions):
     inverse = 1.0 / ROPE_BASE ** (jnp.arange(0, HD, 2).astype(jnp.float32) / HD)
     angles = positions.astype(jnp.float32)[:, None] * inverse[None, :]
-    return jnp.cos(angles), jnp.sin(angles)
-
-
-def rotate(values, cosine, sine):
-    half = HD // 2
-    one, two = values[:, :half], values[:, half:]
-    return jnp.concatenate(
-        [one * cosine - two * sine, two * cosine + one * sine], axis=-1
-    ).astype(jnp.bfloat16)
+    cosine, sine = jnp.cos(angles), jnp.sin(angles)
+    return (
+        jnp.concatenate([cosine, cosine], axis=-1),
+        jnp.concatenate([-sine, sine], axis=-1),
+    )
 
 
 def body(
@@ -650,12 +813,6 @@
     long_blocks = blocks - SHORT_BLOCKS
     rows = 32 * ROWS
 
-    flip = [
-        (((a * 2 + c) * 2 + b), (((1 - a) * 2 + c) * 2 + (1 - b)))
-        for a in range(2)
-        for c in range(2)
-        for b in range(2)
-    ]
     swap = [
         (((a * 2 + c) * 2 + b), (((1 - a) * 2 + (1 - c)) * 2 + (1 - b)))
         for a in range(2)
@@ -664,30 +821,25 @@
         if b != c
     ]
 
-    qkv = attention_in.astype(jnp.bfloat16).reshape(HD, 3, 16, 2, HD)
-    gu = gate_up.astype(jnp.bfloat16).reshape(HD, 2, 16, 2, units)
-
-    def spread(full):
-        mine = lax.dynamic_index_in_dim(full, core, 3, keepdims=False)
-        other = lax.ppermute(mine, ("y_lo", "core", "y_hi"), flip)
-        zero = jnp.where(y_hi == 0, mine, other)
-        one = jnp.where(y_hi == 0, other, mine)
-        both = jnp.stack([zero, one], axis=0)
-        both = jnp.transpose(both, (3, 0, 1, 2, 4))
-        got = lax.all_to_all(both, ("z", "x"), split_axis=0, concat_axis=0, tiled=True)
-        return got.reshape(width, -1)
+    quarter = HD // 2
+
+    def parts_of(weight, sections):
+        piece = lax.dynamic_slice_in_dim(weight, y_lo * quarter, quarter, 0)
+        piece = piece.reshape(quarter, sections, 16, 2, -1)
+        piece = lax.dynamic_index_in_dim(piece, core, 3, keepdims=False).astype(jnp.bfloat16)
+        return jnp.transpose(piece, (2, 0, 1, 3))
+
+    qkv_parts = jnp.pad(parts_of(attention_in, 3), ((0, 0), (0, 0), (0, 0), (0, 128 - HD)))
+    qkv_parts = qkv_parts.reshape(16, quarter, 3 * 128)
+    gu_parts = parts_of(gate_up, 2).reshape(16, quarter, 2 * units)
 
     def own(shard):
         narrow = shard.astype(jnp.bfloat16)
         other = lax.ppermute(narrow, ("y_lo", "core", "y_hi"), swap)
         return jnp.where(y_hi == core, narrow, other)
 
-    w_qkv = spread(qkv)
-    w_gu = spread(gu)
     w_out = own(attention_out)
     w_down = own(down_weight)
-
-    joined = project(rms_norm(states, attention_gain), w_qkv)
 
     own_map = lax.dynamic_slice_in_dim(block_map, y_lo * 8, 8)
     at = jnp.arange(256, dtype=jnp.int32)
@@ -697,12 +849,7 @@
         own_map[:, None] < long_blocks, own_map[:, None] * BLOCK + offset[None], offset % SHORT_LEN
     ).reshape(-1)
     cosine, sine = rope_tables(positions)
-    q = rotate(joined[:, :HD], cosine, sine)
-    k = rotate(joined[:, HD : 2 * HD], cosine, sine)
-    v = joined[:, 2 * HD :].astype(jnp.bfloat16)
-    kv = jnp.stack([k, v])
-    kv_all = lax.all_gather(kv, ("y_lo", "y_hi"), axis=1)
-    kv_all = kv_all.reshape(2, 32, 256, HD)
+    q, kv_all = project(rms_norm(states, attention_gain), qkv_parts, cosine, sine)
 
     offsets = jnp.concatenate([at, at + ROWS])
     prompt = (own_map - long_blocks)[:, None] * (BLOCK // SHORT_LEN) + offsets[None] // SHORT_LEN
@@ -712,14 +859,21 @@
 
     places = jnp.stack([y_hi, y_lo]).astype(jnp.int32)
     attended = attention(
-        q.reshape(8, 256, HD), kv_all[0], kv_all[1], own_map, inverse_map(block_map), places, live
+        q.reshape(8, 256, HD),
+        kv_all.reshape(4, 2, 8, 256, HD),
+        own_map,
+        inverse_map(block_map),
+        places,
+        live,
     ).reshape(rows, HD)
 
-    group = lax.dynamic_index_in_dim(kv_all.reshape(2, 2, 2, 2, 4, 4, ROWS, HD), y_lo, 1, False)
+    group = lax.dynamic_index_in_dim(
+        kv_all.reshape(2, 2, 2, 2, 4, 4, ROWS, HD), y_lo, 1, False
+    )
 
     def cache_rows(target):
         picked = lax.dynamic_index_in_dim(group, target, 2, False)
-        return jnp.transpose(picked, (0, 2, 3, 1, 4, 5)).reshape(2, rows, HD)
+        return jnp.transpose(picked, (1, 2, 3, 0, 4, 5)).reshape(2, rows, HD)
 
     partner = lax.ppermute(
         cache_rows(1 - core),
@@ -728,8 +882,8 @@
     )
     cache = jnp.where(core == y_hi, cache_rows(core), partner)
 
-    residual, normed_two = mix(attended, w_out, states, forward_gain)
-    activated = lift(normed_two, w_gu)
+    residual, normed_two, w_gu = mix(attended, w_out, states, forward_gain, gu_parts)
+    activated = lift(normed_two, w_gu.reshape(width, 2 * units))
     hidden_out = down(activated, w_down, residual)
     return (hidden_out, cache[0], cache[1])
 

time: 507 us -> 383 us (0.76)
  waiting for transfers between devices: 90.7 us -> 0.01 us
  Pallas kernels: 247 us -> 292 us
  starting transfers between devices: 46.8 us -> 5.68 us
  other arithmetic: 45.6 us -> 27.8 us
  between operations: 14.5 us -> 1.03 us
    all_to_all x2 -> x0, waiting for transfers between devices: 61.2 us -> none  [spread(): lax.all_to_all(both, ('z', 'x'), split_axis=0, concat_axis=0, tiled=True)]
    pallas_call x2, Pallas kernels: 104 us -> 150 us  [the longest x1 85.8 us: project(): pl.pallas_call(project_kernel, in_specs=[VM] * 4, out_specs=[VM] * 2, out...]
    all_gather x1 -> x0, waiting for transfers between devices: 29.5 us -> none  [body(): kv_all = lax.all_gather(kv, ('y_lo', 'y_hi'), axis=1)]
    ppermute x1, starting transfers between devices: 17.2 us -> 2.21 us  [body(): lax.ppermute(cache_rows(1 - core), ('core', 'y_hi'), [(b * 2 + b, (1 - b)...]
    all_to_all x2 -> x0, starting transfers between devices: 13.9 us -> none  [spread(): lax.all_to_all(both, ('z', 'x'), split_axis=0, concat_axis=0, tiled=True)]
    ppermute x2 -> x0, starting transfers between devices: 12.2 us -> none  [spread(): other = lax.ppermute(mine, ('y_lo', 'core', 'y_hi'), flip)]
    dynamic_slice x4 -> x2, local copies, waits for them, and re-layouts: 13.5 us -> 4.2 us  [parts_of(): piece = lax.dynamic_slice_in_dim(weight, y_lo * quarter, quarter, 0)]
    another operation x3 -> x0, other arithmetic: 8.61 us -> none  [the longest x2 7.22 us: spread(): both = jnp.stack([zero, one], axis=0)]
  transfers between devices with their start and end apart: 8 -> 3, of which waited for: 3 -> 0; matrix products, arithmetic and copies ran while one was open for 16% -> 10% of each run, Pallas kernels for 50% -> 39%
where the time goes in v3:
time: 383 us; the launch traced here: 376 us
  Pallas kernels  292 us (76%)
  local copies, waits for them, and re-layouts  49.8 us (13%)
  other arithmetic  27.8 us (7%)
  starting transfers between devices  5.68 us (1%)
    pallas_call x1, Pallas kernels, project(): pl.pallas_call(project_kernel, in_specs=[VM] * 4, out_specs=[VM] * 2, out...  85.8 us
    pallas_call x1, Pallas kernels, mix(): pl.pallas_call(mix_kernel, in_specs=[VM] * 5, out_specs=[VM] * 3, out_sha...  63.9 us
    pallas_call x1, Pallas kernels, down(): pl.pallas_call(down_kernel, in_specs=[VM] * 3, out_specs=VM, out_shape=ja...  59 us
    pallas_call x1, Pallas kernels, lift(): pl.pallas_call(lift_kernel, in_specs=[VM] * 2, out_specs=VM, out_shape=ja...  48 us
    pallas_call x1, Pallas kernels, attention(): pl.pallas_call(attention_kernel, grid_spec=pltpu.PrefetchScalarGridSpec(n...  35.2 us
    reshape x2, local copies, waits for them, and re-layouts, parts_of(): piece = piece.reshape(quarter, sections, 16, 2, -1)  9.16 us
    convert_element_type x2, local copies, waits for them, and re-layouts, parts_of(): lax.dynamic_index_in_dim(piece, core, 3, keepdims=False)  7.8 us
  transfers between devices with their start and end apart: 3, of which 0 were waited for; matrix products, arithmetic and copies ran while one was open for 10% of the time, Pallas kernels for 39%

profile of v3, /device:TPU:14, one launch (start us, length us, event | category | flops | bytes accessed | tf_op | source)
XLA Modules:
  0.0 376.3 jit_solution(5344161162577814213)
XLA Ops:
  0.7 0.9 add_multiply_fusion
  1.5 0.5 copy-done.6
  2.0 0.5 broadcast_compare_fusion.1
  2.7 0.7 broadcast_in_dim.52
  3.4 0.1 select_convert_fusion
  3.5 5.6 %fusion.3 = (f32[2,4,4,64,48]{4,3,2,1,0:T(8,128)}, f32[2,4,4,64,48]{4,3,2,1,0:T(8,128)}, f32[2,4,4,64,48]{4,3,2,1,0:T(8,128)S(1)}) fusion(f32[48]{0:T(128)S(1)} %negate_power_fusion, f32[2,4,4,64]{3,2,1,0:T(4,128)S(1)} %select_convert_fusion), kind=kLoop, calls=%fused_computation.22 | loop fusion | flops 196608 | bytes 1188032 | tf_op jit(solution)/shard_map/neg | solution.py:792
  9.1 1.3 pad_maximum_fusion.cos_ref
  10.4 1.0 constant_dynamic-slice_fusion.1
  11.4 5.1 %reshape.351 = bf16[48,3,16,2,96]{4,3,2,1,0:T(2,128)(2,1)} reshape(bf16[48,9216]{1,0:T(8,128)(2,1)} %constant_dynamic-slice_fusion.1) | data formatting | bytes 1769472 | tf_op jit(solution)/shard_map/reshape | solution.py:828
  16.5 2.5 dynamic-slice_convert_fusion.1
  19.1 0.4 copy.52
  19.5 1.4 pad.4.clone
  20.9 3.1 reshape.352.part_ref
  24.0 1.2 fusion
  25.2 2.9 pad_maximum_fusion.1.sin_ref
  28.1 0.9 fusion.2.x_ref
  29.0 85.8 %project.1 = (bf16[2,4,4,64,96]{4,3,2,1,0:T(8,128)(2,1)}, bf16[4,2,2,4,4,64,96]{6,5,4,3,2,1,0:T(8,128)(2,1)}) custom-call(bf16[64,3072]{1,0:T(8,128)(2,1)} %fusion.2.x_ref, bf16[16,48,384]{2,1,0:T(8,128)(2,1)} %reshape.352.part_ref, f32[2,4,4,64,96]{4,3,2,1,0:T(8,128)} %pad_maximum_fusion.cos_ref, f32[2,4,4,64,96]{4,3,2,1,0:T(8,128)} %pad_maximum_fusion.1.sin_ref), custom_call_target="tpu_custom_call" | custom-call | tf_op jit(solution)/shard_map/project/pallas_call | solution.py:756
  114.9 2.8 dynamic-slice_bitcast_fusion.1
  117.6 1.0 copy.43
  118.6 2.2 copy.44
  120.8 2.2 collective-permute-start.2
  123.0 2.2 convert_element_type.57
  125.2 1.6 collective-permute-start
  126.9 3.3 convert_element_type.60
  130.1 1.8 collective-permute-start.1
  132.0 0.7 select_reduce_fusion.1.slot_of
  132.7 3.2 constant_dynamic-slice_fusion
  135.9 4.0 %reshape.356 = bf16[48,2,16,2,256]{4,3,2,1,0:T(2,128)(2,1)} reshape(bf16[48,16384]{1,0:T(8,128)(2,1)} %constant_dynamic-slice_fusion) | data formatting | bytes 3145728 | tf_op jit(solution)/shard_map/reshape | solution.py:828
  140.0 0.2 select_reduce_fusion
  140.1 0.6 compare_convert_fusion.live_ref
  140.8 0.7 pad_add_fusion.1.half_ref
  141.4 35.2 %attention.1 = bf16[8,256,96]{2,1,0:T(8,128)(2,1)} custom-call(s32[8]{0:T(128)} %copy-done.6, s32[16]{0:T(128)} %select_reduce_fusion.1.slot_of, s32[2]{0:T(128)} %pad_add_fusion.1.half_ref, bf16[8,256,96]{2,1,0:T(8,128)(2,1)} %bitcast.45, bf16[4,2,8,256,96]{4,3,2,1,0:T(8,128)(2,1)} %bitcast.42, f32[8,1,512]{2,1,0:T(1,128)} %compare_convert_fusion.live_ref), custom_call_target="tpu_custom_call" | custom-call | flops 8000000000 | bytes 8000000 | tf_op jit(solution)/shard_map/attention/pallas_call | solution.py:134
  176.6 5.3 %dynamic-slice_convert_fusion = bf16[48,2,16,1,256]{4,3,2,1,0:T(2,128)(2,1)} fusion(bf16[48,2,16,2,256]{4,3,2,1,0:T(2,128)(2,1)} %reshape.356, s32[]{:T(128)S(6)} %select_n.162), kind=kLoop, calls=%fused_computation | loop fusion | bytes 1572868 | tf_op jit(solution)/shard_map/convert_element_type | solution.py:829
  181.9 2.4 copy.41
  184.4 0.2 copy.55
  184.6 1.6 copy.39
  186.2 3.1 reshape.357.part_ref
  189.3 2.2 broadcast_select_fusion.1.right_ref
  191.5 63.9 %mix.1 = (f32[64,3072]{1,0:T(8,128)}, bf16[64,3072]{1,0:T(8,128)(2,1)}, bf16[16,4,48,512]{3,2,1,0:T(8,128)(2,1)}) custom-call(bf16[2,4,4,64,96]{4,3,2,1,0:T(8,128)(2,1)} %bitcast.43, bf16[96,3072]{1,0:T(8,128)(2,1)} %broadcast_select_fusion.1.right_ref, bf16[64,3072]{1,0:T(8,128)(2,1)} %base_ref.1, f32[1,3072]{1,0:T(1,128)} %bitcast.44, ...), custom_call_target="tpu_custom_call" | custom-call | tf_op jit(solution)/shard_map/mix/pallas_call | solution.py:510
  255.4 48.0 %lift.1.left_ref = bf16[2,4,4,64,256]{4,3,2,1,0:T(8,128)(2,1)} custom-call(bf16[64,3072]{1,0:T(8,128)(2,1)} %get-tuple-element.10.x_ref, bf16[3072,512]{1,0:T(8,128)(2,1)} %bitcast.38), custom_call_target="tpu_custom_call" | custom-call | tf_op jit(solution)/shard_map/lift/pallas_call | solution.py:775
  303.4 2.2 copy.45
  305.7 1.3 bitcast_select_fusion
  307.0 1.0 slice_bitcast_fusion
  308.0 2.0 copy.46
  310.0 2.0 copy.47
  312.0 3.2 broadcast_select_fusion.right_ref
  315.3 59.0 %down.1 = bf16[64,3072]{1,0:T(8,128)(2,1)} custom-call(bf16[2,4,4,64,256]{4,3,2,1,0:T(8,128)(2,1)} %lift.1.left_ref, bf16[256,3072]{1,0:T(8,128)(2,1)} %broadcast_select_fusion.right_ref, f32[64,3072]{1,0:T(8,128)} %get-tuple-element.12.base_ref), custom_call_target="tpu_custom_call" | custom-call | tf_op jit(solution)/shard_map/down/pallas_call | solution.py:527
  374.3 1.8 copy.58
  (25 shorter events, 0.3 us)
Async XLA Ops:
  0.6 9.8 %copy-start = (f32[96,9216]{1,0:T(8,128)S(1)}, f32[96,9216]{1,0:T(8,128)}, u32[]{:S(2)}) copy-start(f32[96,9216]{1,0:T(8,128)} %param.12) | copy-start | bytes 10616836
  1.5 0.5 copy-start.6
  25.2 3.0 copy-start.2
  25.2 3.0 copy-start.3
  120.8 182.6 %collective-permute-start.2 = (bf16[2,2048,96]{1,2,0:T(8,128)(2,1)}, bf16[2,2048,96]{1,2,0:T(8,128)(2,1)}, u32[]{:S(2)}, u32[]{:S(2)}) collective-permute-start(bf16[2,2048,96]{1,2,0:T(8,128)(2,1)} %copy.44), channel_id=1, source_target_pairs={{0,32},{33,1},{2,34},{35,3},{4,36},{37,5},{6,38},{39,7},{8,40},{41... | collective-permute-start | bytes 2359304 | tf_op jit(solution)/shard_map/ppermute | solution.py:878
  125.2 6.8 %copy-start.5 = (s32[16]{0:T(128)S(1)}, s32[16]{0:T(128)}, u32[]{:S(2)}) copy-start(s32[16]{0:T(128)} %param.16) | copy-start | bytes 196
  125.2 64.1 %collective-permute-start = (bf16[96,3072]{1,0:T(8,128)(2,1)}, bf16[96,3072]{1,0:T(8,128)(2,1)}, u32[]{:S(2)}, u32[]{:S(2)}) collective-permute-start(bf16[96,3072]{1,0:T(8,128)(2,1)} %convert_element_type.57), channel_id=1, source_target_pairs={{1,96},{32,65},{65,32},{96,1},{3,98},{34,67},{67,34},{98,3},{5,100... | collective-permute-start | bytes 1769480 | tf_op jit(solution)/shard_map/ppermute | solution.py:838
  130.1 181.9 %collective-permute-start.1 = (bf16[256,3072]{1,0:T(8,128)(2,1)}, bf16[256,3072]{1,0:T(8,128)(2,1)}, u32[]{:S(2)}, u32[]{:S(2)}) collective-permute-start(bf16[256,3072]{1,0:T(8,128)(2,1)} %convert_element_type.60), channel_id=1, source_target_pairs={{1,96},{32,65},{65,32},{96,1},{3,98},{34,67},{67,34},{98,3},{5,100... | collective-permute-start | bytes 4718600 | tf_op jit(solution)/shard_map/ppermute | solution.py:838
  135.8 4.1 %copy-start.4 = (s32[32]{0:T(128)S(1)}, s32[32]{0:T(128)}, u32[]{:S(2)}) copy-start(s32[32]{0:T(128)} %param.17) | copy-start | bytes 388
  181.9 2.4 copy-start.1

commit v4 on v3

--- a/solution.py
+++ b/solution.py
@@ -783,13 +783,143 @@
     )(x, w).reshape(32 * ROWS, units)
 
 
-def rope_tables(positions):
-    inverse = 1.0 / ROPE_BASE ** (jnp.arange(0, HD, 2).astype(jnp.float32) / HD)
-    angles = positions.astype(jnp.float32)[:, None] * inverse[None, :]
-    cosine, sine = jnp.cos(angles), jnp.sin(angles)
-    return (
-        jnp.concatenate([cosine, cosine], axis=-1),
-        jnp.concatenate([-sine, sine], axis=-1),
+def rope_constants():
+    inverse = 1.0 / ROPE_BASE ** (np.arange(0, HD, 2) / HD)
+
+    def table(positions):
+        angles = np.asarray(positions, np.float64)[:, None] * inverse[None, :]
+        cosine, sine = np.cos(angles), np.sin(angles)
+        return np.stack(
+            [np.concatenate([cosine, cosine], 1), np.concatenate([-sine, sine], 1)]
+        ).astype(np.float32)
+
+    blocks = np.arange(16)
+    base = table(np.where(blocks < 16 - SHORT_BLOCKS, blocks * BLOCK, 0))
+    at = np.arange(256)
+    at = (at // ROWS) * (2 * ROWS) + at % ROWS
+    inner = np.stack(
+        [
+            np.stack([table(at + h * ROWS), table((at + h * ROWS) % SHORT_LEN)])
+            for h in range(2)
+        ]
+    )
+    return base[:, :, None, :], inner
+
+
+PREP = 4
+
+
+def prep_kernel(
+    own_map,
+    place,
+    x_ref,
+    gain_ref,
+    *refs,
+):
+    wide = refs[:5]
+    out_ref, down_ref, base_ref, inner_ref = refs[5:9]
+    normed_ref, qkv_ref, gu_ref, wout_ref, wdown_ref, cos_ref, sin_ref = refs[9:]
+    step = pl.program_id(0)
+    core = place[1]
+    normed_ref[...] = rms_norm(x_ref[...], gain_ref[...])
+    wout_ref[...] = out_ref[...].astype(jnp.bfloat16)
+    wdown_ref[...] = down_ref[...].astype(jnp.bfloat16)
+    units = gu_ref.shape[2] // 2
+    blank = jnp.zeros((qkv_ref.shape[1], 128 - HD), jnp.float32)
+    for j in range(4):
+        for k in range(2):
+            cols = pl.ds(pl.multiple_of((2 * j + core) * units, 128), units)
+            gu_ref[j, :, k * units : (k + 1) * units] = wide[3 + k][:, cols].astype(
+                jnp.bfloat16
+            )
+        for k in range(3):
+            even = wide[k][:, 2 * j * HD : (2 * j + 1) * HD]
+            odd = wide[k][:, (2 * j + 1) * HD : (2 * j + 2) * HD]
+            value = jnp.concatenate([jnp.where(core == 0, even, odd), blank], axis=1)
+            qkv_ref[j, :, k * 128 : (k + 1) * 128] = value.astype(jnp.bfloat16)
+    for j in range(2):
+        logical = own_map[2 * step + j]
+        kind = (logical >= base_ref.shape[1] - SHORT_BLOCKS).astype(jnp.int32)
+        cos_at, sin_at = base_ref[0, logical], base_ref[1, logical]
+        cos_in, sin_in = inner_ref[0, kind, 0], inner_ref[0, kind, 1]
+        rows = pl.ds(j * 256, 256)
+        cos_ref[rows, :] = cos_at * cos_in - sin_at * sin_in
+        sin_ref[rows, :] = sin_at * cos_in + cos_at * sin_in
+
+
+def prep(states, gain, attention_in, attention_out, gate_up, down_weight, own_map, place):
+    width = states.shape[1]
+    units = down_weight.shape[0]
+    quarter = HD // 2
+    base, inner = rope_constants()
+
+    def wide(columns, section):
+        return pl.BlockSpec(
+            (quarter, columns), lambda i, own, at: (at[0], section * PREP + i)
+        )
+
+    def across(shape):
+        return pl.BlockSpec(shape, lambda i, *_: (0, i))
+
+    def along(shape):
+        return pl.BlockSpec(shape, lambda i, *_: (i,) + (0,) * (len(shape) - 1))
+
+    def whole(array):
+        return pl.BlockSpec(array.shape, lambda i, *_: (0,) * array.ndim)
+
+    gain = gain.reshape(1, width)
+    rows = 32 * ROWS
+    return pl.pallas_call(
+        prep_kernel,
+        grid_spec=pltpu.PrefetchScalarGridSpec(
+            num_scalar_prefetch=2,
+            grid=(PREP,),
+            in_specs=[along((ROWS // PREP, width)), whole(gain)]
+            + [wide(8 * HD, k) for k in range(3)]
+            + [wide(8 * units, k) for k in range(2)]
+            + [
+                across((HD, width // PREP)),
+                along((units // PREP, width)),
+                whole(base),
+                pl.BlockSpec(
+                    (1,) + inner.shape[1:], lambda i, own, at: (at[2], 0, 0, 0, 0)
+                ),
+            ],
+            out_specs=[
+                along((ROWS // PREP, width)),
+                along((16 // PREP, quarter, 3 * 128)),
+                along((16 // PREP, quarter, 2 * units)),
+                across((HD, width // PREP)),
+                along((units // PREP, width)),
+                along((rows // PREP, HD)),
+                along((rows // PREP, HD)),
+            ],
+        ),
+        out_shape=[
+            jax.ShapeDtypeStruct((ROWS, width), jnp.bfloat16),
+            jax.ShapeDtypeStruct((16, quarter, 3 * 128), jnp.bfloat16),
+            jax.ShapeDtypeStruct((16, quarter, 2 * units), jnp.bfloat16),
+            jax.ShapeDtypeStruct((HD, width), jnp.bfloat16),
+            jax.ShapeDtypeStruct((units, width), jnp.bfloat16),
+            jax.ShapeDtypeStruct((rows, HD), jnp.float32),
+            jax.ShapeDtypeStruct((rows, HD), jnp.float32),
+        ],
+        compiler_params=pltpu.CompilerParams(vmem_limit_bytes=48 * 1024 * 1024),
+        name="prep",
+    )(
+        own_map,
+        place,
+        states,
+        gain,
+        attention_in,
+        attention_in,
+        attention_in,
+        gate_up,
+        gate_up,
+        attention_out,
+        down_weight,
+        base,
+        inner,
     )
 
 
@@ -821,35 +951,28 @@
         if b != c
     ]
 
-    quarter = HD // 2
-
-    def parts_of(weight, sections):
-        piece = lax.dynamic_slice_in_dim(weight, y_lo * quarter, quarter, 0)
-        piece = piece.reshape(quarter, sections, 16, 2, -1)
-        piece = lax.dynamic_index_in_dim(piece, core, 3, keepdims=False).astype(jnp.bfloat16)
-        return jnp.transpose(piece, (2, 0, 1, 3))
-
-    qkv_parts = jnp.pad(parts_of(attention_in, 3), ((0, 0), (0, 0), (0, 0), (0, 128 - HD)))
-    qkv_parts = qkv_parts.reshape(16, quarter, 3 * 128)
-    gu_parts = parts_of(gate_up, 2).reshape(16, quarter, 2 * units)
-
-    def own(shard):
-        narrow = shard.astype(jnp.bfloat16)
+    own_map = lax.dynamic_slice_in_dim(block_map, y_lo * 8, 8)
+    normed, qkv_parts, gu_parts, w_out, w_down, cosine, sine = prep(
+        states,
+        attention_gain,
+        attention_in,
+        attention_out,
+        gate_up,
+        down_weight,
+        own_map,
+        jnp.stack([y_lo, core, y_hi]).astype(jnp.int32),
+    )
+
+    def own(narrow):
         other = lax.ppermute(narrow, ("y_lo", "core", "y_hi"), swap)
         return jnp.where(y_hi == core, narrow, other)
 
-    w_out = own(attention_out)
-    w_down = own(down_weight)
-
-    own_map = lax.dynamic_slice_in_dim(block_map, y_lo * 8, 8)
+    w_out = own(w_out)
+    w_down = own(w_down)
+
     at = jnp.arange(256, dtype=jnp.int32)
     at = (at // ROWS) * (2 * ROWS) + at % ROWS
-    offset = at + y_hi * ROWS
-    positions = jnp.where(
-        own_map[:, None] < long_blocks, own_map[:, None] * BLOCK + offset[None], offset % SHORT_LEN
-    ).reshape(-1)
-    cosine, sine = rope_tables(positions)
-    q, kv_all = project(rms_norm(states, attention_gain), qkv_parts, cosine, sine)
+    q, kv_all = project(normed, qkv_parts, cosine, sine)
 
     offsets = jnp.concatenate([at, at + ROWS])
     prompt = (own_map - long_blocks)[:, None] * (BLOCK // SHORT_LEN) + offsets[None] // SHORT_LEN

time: 383 us -> 337 us (0.88)
  local copies, waits for them, and re-layouts: 49.8 us -> 15.9 us
  other arithmetic: 27.8 us -> 5.33 us
  Pallas kernels: 292 us -> 304 us
    reshape x4 -> x0, local copies, waits for them, and re-layouts: 15.4 us -> none  [the longest x2 9.16 us: parts_of(): piece = piece.reshape(quarter, sections, 16, 2, -1)]
    convert_element_type x2 -> x0, local copies, waits for them, and re-layouts: 7.8 us -> none  [parts_of(): lax.dynamic_index_in_dim(piece, core, 3, keepdims=False)]
    pallas_call x0 -> x1, Pallas kernels: none -> 6.5 us  [prep(): pl.pallas_call(prep_kernel, grid_spec=pltpu.PrefetchScalarGridSpec(num_sc...]
    convert_element_type x4 -> x0, other arithmetic: 6.45 us -> none  [the longest x2 5.46 us: own(): narrow = shard.astype(jnp.bfloat16)]
    pallas_call x1, Pallas kernels: 63.9 us -> 70 us  [mix(): pl.pallas_call(mix_kernel, in_specs=[VM] * 5, out_specs=[VM] * 3, out_sha...]
    neg x1 -> x0, other arithmetic: 5.59 us -> none  [rope_tables(): -sine]
    pallas_call x1, Pallas kernels: 85.8 us -> 91 us  [project(): pl.pallas_call(project_kernel, in_specs=[VM] * 4, out_specs=[VM] * 2, out...]
    unnamed x20 -> x29, local copies, waits for them, and re-layouts: 6.95 us -> 11.8 us
  transfers between devices with their start and end apart: 3 -> 3, of which waited for: 0 -> 0; matrix products, arithmetic and copies ran while one was open for 10% -> 3% of each run, Pallas kernels for 39% -> 72%
where the time goes in v4:
time: 337 us; the launch traced here: 331 us
  Pallas kernels  304 us (90%)
  local copies, waits for them, and re-layouts  15.9 us (5%)
  starting transfers between devices  5.55 us (2%)
  other arithmetic  5.33 us (2%)
    pallas_call x1, Pallas kernels, project(): pl.pallas_call(project_kernel, in_specs=[VM] * 4, out_specs=[VM] * 2, out...  91 us
    pallas_call x1, Pallas kernels, mix(): pl.pallas_call(mix_kernel, in_specs=[VM] * 5, out_specs=[VM] * 3, out_sha...  70 us
    pallas_call x1, Pallas kernels, down(): pl.pallas_call(down_kernel, in_specs=[VM] * 3, out_specs=VM, out_shape=ja...  59.5 us
    pallas_call x1, Pallas kernels, lift(): pl.pallas_call(lift_kernel, in_specs=[VM] * 2, out_specs=VM, out_shape=ja...  45.8 us
    pallas_call x1, Pallas kernels, attention(): pl.pallas_call(attention_kernel, grid_spec=pltpu.PrefetchScalarGridSpec(n...  31.2 us
    unnamed x29, local copies, waits for them, and re-layouts  11.8 us
  transfers between devices with their start and end apart: 3, of which 0 were waited for; matrix products, arithmetic and copies ran while one was open for 3% of the time, Pallas kernels for 72%

profile of v4, /device:TPU:14, one launch (start us, length us, event | category | flops | bytes accessed | tf_op | source)
XLA Modules:
  0.0 331.5 jit_solution(16551360670411266643)
XLA Ops:
  0.6 0.7 add_multiply_fusion
  1.4 0.0 copy-start.9
  1.4 0.1 pad_add_fusion.2.place
  1.5 1.0 copy-done
  2.5 1.2 copy-done.3
  3.7 0.7 copy-done.7
  4.4 0.7 copy-done.8
  5.1 6.5 %prep.1 = (bf16[64,3072]{1,0:T(8,128)(2,1)S(1)}, bf16[16,48,384]{2,1,0:T(8,128)(2,1)S(1)}, bf16[16,48,512]{2,1,0:T(8,128)(2,1)S(1)}, bf16[96,3072]{1,0:T(8,128)(...) custom-call(s32[8]{0:T(128)S(1)} %get-tuple-element.37.own_map, ...), custom_call_target="tpu_custom_call" | custom-call | tf_op jit(solution)/shard_map/prep/pallas_call | solution.py:872
  11.6 0.0 copy-done.9
  11.6 1.0 copy-done.1
  12.6 1.0 copy-done.2
  13.7 0.9 copy-done.4
  14.6 0.8 copy-done.5
  15.4 0.7 copy-done.6
  16.1 1.5 collective-permute-start
  17.6 1.8 collective-permute-start.1
  19.5 91.0 %project.1 = (bf16[2,4,4,64,96]{4,3,2,1,0:T(8,128)(2,1)}, bf16[4,2,2,4,4,64,96]{6,5,4,3,2,1,0:T(8,128)(2,1)}) custom-call(bf16[64,3072]{1,0:T(8,128)(2,1)} %copy-done.6, bf16[16,48,384]{2,1,0:T(8,128)(2,1)} %copy-done.5, f32[2,4,4,64,96]{4,3,2,1,0:T(8,128)} %bitcast.31, f32[2,4,4,64,96]{4,3,2,1,0:T(8,128)} %bitcast.32), custom_call_target="tpu_custom_call" | custom-call | tf_op jit(solution)/shard_map/project/pallas_call | solution.py:756
  110.5 1.7 dynamic-slice_bitcast_fusion.1
  112.2 0.0 copy-start.12
  112.2 0.0 copy-start.11
  112.2 0.1 copy.31
  112.3 0.5 copy.32
  112.8 2.2 collective-permute-start.2
  115.1 0.6 pad_add_fusion.1.half_ref
  115.7 0.0 copy-done.12
  115.7 0.6 select_reduce_fusion.1.slot_of
  116.3 0.1 broadcast_add_fusion
  116.4 0.0 copy-done.11
  116.4 0.2 select_reduce_fusion
  116.6 0.6 compare_convert_fusion.live_ref
  117.2 31.2 %attention.1 = bf16[8,256,96]{2,1,0:T(8,128)(2,1)} custom-call(s32[8]{0:T(128)} %copy-done.9, s32[16]{0:T(128)} %select_reduce_fusion.1.slot_of, s32[2]{0:T(128)} %pad_add_fusion.1.half_ref, bf16[8,256,96]{2,1,0:T(8,128)(2,1)} %bitcast.40, bf16[4,2,8,256,96]{4,3,2,1,0:T(8,128)(2,1)} %bitcast.37, f32[8,1,512]{2,1,0:T(1,128)} %compare_convert_fusion.live_ref), custom_call_target="tpu_custom_call" | custom-call | flops 8000000000 | bytes 8000000 | tf_op jit(solution)/shard_map/attention/pallas_call | solution.py:134
  148.4 0.1 copy.29
  148.5 0.0 collective-permute-done
  148.5 0.9 broadcast_select_fusion.1.right_ref
  149.4 70.0 %mix.1 = (f32[64,3072]{1,0:T(8,128)}, bf16[64,3072]{1,0:T(8,128)(2,1)}, bf16[16,4,48,512]{3,2,1,0:T(8,128)(2,1)}) custom-call(bf16[2,4,4,64,96]{4,3,2,1,0:T(8,128)(2,1)} %bitcast.38, bf16[96,3072]{1,0:T(8,128)(2,1)} %broadcast_select_fusion.1.right_ref, bf16[64,3072]{1,0:T(8,128)(2,1)} %base_ref.1, f32[1,3072]{1,0:T(1,128)} %bitcast.39, ...), custom_call_target="tpu_custom_call" | custom-call | tf_op jit(solution)/shard_map/mix/pallas_call | solution.py:510
  219.4 45.8 %lift.1.left_ref = bf16[2,4,4,64,256]{4,3,2,1,0:T(8,128)(2,1)} custom-call(bf16[64,3072]{1,0:T(8,128)(2,1)} %get-tuple-element.23.x_ref, bf16[3072,512]{1,0:T(8,128)(2,1)} %bitcast.35), custom_call_target="tpu_custom_call" | custom-call | tf_op jit(solution)/shard_map/lift/pallas_call | solution.py:775
  265.1 0.0 collective-permute-done.2
  265.1 1.6 copy.33
  266.7 0.2 bitcast_select_fusion
  266.9 0.0 copy-start.10
  266.9 0.1 slice_bitcast_fusion
  267.0 1.0 copy.35
  267.9 1.0 copy.34
  268.9 0.0 collective-permute-done.1
  268.9 0.0 copy-done.10
  268.9 1.3 broadcast_select_fusion.right_ref
  270.2 59.5 %down.1 = bf16[64,3072]{1,0:T(8,128)(2,1)} custom-call(bf16[2,4,4,64,256]{4,3,2,1,0:T(8,128)(2,1)} %lift.1.left_ref, bf16[256,3072]{1,0:T(8,128)(2,1)} %broadcast_select_fusion.right_ref, f32[64,3072]{1,0:T(8,128)} %get-tuple-element.26.base_ref), custom_call_target="tpu_custom_call" | custom-call | tf_op jit(solution)/shard_map/down/pallas_call | solution.py:527
  329.7 1.8 copy.39
  (11 shorter events, 0.0 us)
Async XLA Ops:
  1.4 10.2 %copy-start.9 = (s32[8]{0:T(128)}, s32[8]{0:T(128)S(1)}, u32[]{:S(2)}) copy-start(s32[8]{0:T(128)S(1)} %get-tuple-element.37.own_map) | copy-start | bytes 100
  1.4 1.0 copy-start
  2.4 1.2 copy-start.3
  3.7 0.7 copy-start.7
  4.4 0.7 copy-start.8
  11.6 1.0 copy-start.1
  12.6 1.0 copy-start.2
  13.7 0.9 copy-start.4
  14.6 0.8 copy-start.5
  15.4 0.7 copy-start.6
  16.1 132.4 %collective-permute-start = (bf16[96,3072]{1,0:T(8,128)(2,1)S(1)}, bf16[96,3072]{1,0:T(8,128)(2,1)}, u32[]{:S(2)}, u32[]{:S(2)}) collective-permute-start(bf16[96,3072]{1,0:T(8,128)(2,1)S(1)} %get-tuple-element.21), channel_id=1, source_target_pairs={{1,96},{32,65},{65,32},{96,1},{3,98},{34,67},{67,34},{98,3},{5,100... | collective-permute-start | bytes 1769480 | tf_op jit(solution)/shard_map/ppermute | solution.py:967
  17.6 251.3 %collective-permute-start.1 = (bf16[256,3072]{1,0:T(8,128)(2,1)}, bf16[256,3072]{1,0:T(8,128)(2,1)}, u32[]{:S(2)}, u32[]{:S(2)}) collective-permute-start(bf16[256,3072]{1,0:T(8,128)(2,1)} %get-tuple-element.25), channel_id=1, source_target_pairs={{1,96},{32,65},{65,32},{96,1},{3,98},{34,67},{67,34},{98,3},{5,100... | collective-permute-start | bytes 4718600 | tf_op jit(solution)/shard_map/ppermute | solution.py:967
  112.2 3.4 %copy-start.12 = (s32[16]{0:T(128)S(1)}, s32[16]{0:T(128)}, u32[]{:S(2)}) copy-start(s32[16]{0:T(128)} %param.18) | copy-start | bytes 196
  112.2 4.2 %copy-start.11 = (s32[32]{0:T(128)S(1)}, s32[32]{0:T(128)}, u32[]{:S(2)}) copy-start(s32[32]{0:T(128)} %param.19) | copy-start | bytes 388
  112.8 152.3 %collective-permute-start.2 = (bf16[2,2048,96]{1,2,0:T(8,128)(2,1)S(1)}, bf16[2,2048,96]{1,2,0:T(8,128)(2,1)}, u32[]{:S(2)}, u32[]{:S(2)}) collective-permute-start(bf16[2,2048,96]{1,2,0:T(8,128)(2,1)S(1)} %copy.32), channel_id=1, source_target_pairs={{0,32},{33,1},{2,34},{35,3},{4,36},{37,5},{6,38},{39,7},{8,40},{41... | collective-permute-start | bytes 2359304 | tf_op jit(solution)/shard_map/ppermute | solution.py:1001
  266.9 2.0 copy-start.10

commit v5 on v4

--- a/solution.py
+++ b/solution.py
@@ -291,7 +291,8 @@
         return (far, right, left, me)[step]
 
     swaps = {}
-    for step in range(4):
+
+    def hand_over(step):
         for half in range(2):
             at = half * 4 + step
             make(other.at[half, step], None, half, 1 - core, big_at(half, step))
@@ -306,7 +307,8 @@
                 )
             )
 
-    hook(0)
+    hand_over(0)
+    hand_over(1)
     first = {}
     second = {}
     for half in range(2):
@@ -324,6 +326,9 @@
                     peer,
                 )
             )
+    hand_over(2)
+    hand_over(3)
+    hook(0)
     for side in range(2):
         for half in range(2):
             _, right, left, _ = rings[half]
@@ -535,7 +540,7 @@
     )(left.reshape(2, 4, 4, ROWS, -1), right, base)
 
 
-def gather_steps(x_ref, buf, sems, use, hook):
+def gather_steps(x_ref, buf, sems, use, hook, eager):
     core = lax.axis_index("core")
     axes = ("z", "x")
     rings = (ring("z"), ring("x"))
@@ -606,10 +611,15 @@
             )
         cores[half, 3] = go(push(whole, whole, sems[1], half * 4 + 3, "core", 1 - core))
     hook(2)
-    for half in range(2):
-        for i in range(4):
-            cores[half, i].wait_recv()
-        use(half, rings[half][0])
+
+    def use_own():
+        for half in range(2):
+            for i in range(4):
+                cores[half, i].wait_recv()
+            use(half, rings[half][0])
+
+    if not eager:
+        use_own()
     four = {}
     fives = {}
     for half in range(2):
@@ -622,6 +632,9 @@
             fives[half, side] = go(
                 push(chunk, chunk, sems[5], half * 4 + side, "core", 1 - core)
             )
+    if eager:
+        hook(3)
+        use_own()
     for half in range(2):
         _, right, left, _ = rings[half]
         for side, frm in ((0, left), (1, right)):
@@ -649,10 +662,10 @@
     ]
 
 
-def gather_scope(x_ref, scratch, use, hook=lambda at: None):
+def gather_scope(x_ref, scratch, use, hook=lambda at: None, eager=False):
     buf = scratch[0]
     sems = [(scratch[1 + 2 * i], scratch[2 + 2 * i]) for i in range(6)]
-    gather_steps(x_ref, buf, sems, use, hook)
+    gather_steps(x_ref, buf, sems, use, hook, eager)
 
 
 def project_kernel(x_ref, part_ref, cos_ref, sin_ref, q_ref, kv_ref, full_ref, *scratch):
@@ -669,8 +682,9 @@
             spread.send()
         elif at == 1:
             spread.along()
+        elif at == 2:
+            spread.relay()
         else:
-            spread.relay()
             spread.arrive()
 
     def window(half, big):
@@ -722,7 +736,7 @@
         started.append((half, big, pushes))
         forward(index)
 
-    gather_scope(x_ref, scratch[:13], use, hook)
+    gather_scope(x_ref, scratch[:13], use, hook, True)
     forward(8)
     for now in passed:
         for copy in now:

time: 337 us -> 326 us (0.967); the launches traced: 331 us -> 324 us
  Pallas kernels: 304 us -> 296 us
    pallas_call x1, Pallas kernels: 70 us -> 62.8 us  [mix(): pl.pallas_call(mix_kernel, in_specs=[VM] * 5, out_specs=[VM] * 3, out_sha...]
    pallas_call x1, Pallas kernels: 31.2 us -> 36.9 us  [attention(): pl.pallas_call(attention_kernel, grid_spec=pltpu.PrefetchScalarGridSpec(n...]
    pallas_call x1, Pallas kernels: 59.5 us -> 55 us  [down(): pl.pallas_call(down_kernel, in_specs=[VM] * 3, out_specs=VM, out_shape=ja...]
where the time goes in v5:
time: 326 us; the launch traced here: 324 us
  Pallas kernels  296 us (91%)
  local copies, waits for them, and re-layouts  15.9 us (5%)
  starting transfers between devices  6.28 us (2%)
  other arithmetic  5.33 us (2%)
    pallas_call x1, Pallas kernels, project(): pl.pallas_call(project_kernel, in_specs=[VM] * 4, out_specs=[VM] * 2, out...  88.8 us
    pallas_call x1, Pallas kernels, mix(): pl.pallas_call(mix_kernel, in_specs=[VM] * 5, out_specs=[VM] * 3, out_sha...  62.8 us
    pallas_call x1, Pallas kernels, down(): pl.pallas_call(down_kernel, in_specs=[VM] * 3, out_specs=VM, out_shape=ja...  55 us
    pallas_call x1, Pallas kernels, lift(): pl.pallas_call(lift_kernel, in_specs=[VM] * 2, out_specs=VM, out_shape=ja...  45.8 us
    pallas_call x1, Pallas kernels, attention(): pl.pallas_call(attention_kernel, grid_spec=pltpu.PrefetchScalarGridSpec(n...  36.9 us
    unnamed x29, local copies, waits for them, and re-layouts  11.8 us
  transfers between devices with their start and end apart: 3, of which 0 were waited for; matrix products, arithmetic and copies ran while one was open for 3% of the time, Pallas kernels for 72%

profile of v5, /device:TPU:14, one launch (start us, length us, event | category | flops | bytes accessed | tf_op | source)
XLA Modules:
  0.0 324.1 jit_solution(13060869376935506824)
XLA Ops:
  0.6 0.7 add_multiply_fusion
  1.4 0.0 copy-start.9
  1.4 0.1 pad_add_fusion.2.place
  1.5 1.0 copy-done
  2.5 1.2 copy-done.3
  3.7 0.7 copy-done.7
  4.4 0.7 copy-done.8
  5.1 6.5 %prep.1 = (bf16[64,3072]{1,0:T(8,128)(2,1)S(1)}, bf16[16,48,384]{2,1,0:T(8,128)(2,1)S(1)}, bf16[16,48,512]{2,1,0:T(8,128)(2,1)S(1)}, bf16[96,3072]{1,0:T(8,128)(...) custom-call(s32[8]{0:T(128)S(1)} %get-tuple-element.37.own_map, ...), custom_call_target="tpu_custom_call" | custom-call | tf_op jit(solution)/shard_map/prep/pallas_call | solution.py:886
  11.6 0.0 copy-done.9
  11.6 1.0 copy-done.1
  12.6 1.0 copy-done.2
  13.7 0.9 copy-done.4
  14.6 0.8 copy-done.5
  15.4 0.7 copy-done.6
  16.1 1.5 collective-permute-start
  17.6 1.8 collective-permute-start.1
  19.5 88.8 %project.1 = (bf16[2,4,4,64,96]{4,3,2,1,0:T(8,128)(2,1)}, bf16[4,2,2,4,4,64,96]{6,5,4,3,2,1,0:T(8,128)(2,1)}) custom-call(bf16[64,3072]{1,0:T(8,128)(2,1)} %copy-done.6, bf16[16,48,384]{2,1,0:T(8,128)(2,1)} %copy-done.5, f32[2,4,4,64,96]{4,3,2,1,0:T(8,128)} %bitcast.31, f32[2,4,4,64,96]{4,3,2,1,0:T(8,128)} %bitcast.32), custom_call_target="tpu_custom_call" | custom-call | tf_op jit(solution)/shard_map/project/pallas_call | solution.py:770
  108.3 1.7 dynamic-slice_bitcast_fusion.1
  110.0 0.0 copy-start.12
  110.0 0.0 copy-start.11
  110.1 0.1 copy.31
  110.1 0.5 copy.32
  110.7 2.9 collective-permute-start.2
  113.6 0.6 pad_add_fusion.1.half_ref
  114.2 0.0 copy-done.12
  114.2 0.6 select_reduce_fusion.1.slot_of
  114.9 0.1 broadcast_add_fusion
  114.9 0.0 copy-done.11
  114.9 0.2 select_reduce_fusion
  115.1 0.6 compare_convert_fusion.live_ref
  115.7 36.9 %attention.1 = bf16[8,256,96]{2,1,0:T(8,128)(2,1)} custom-call(s32[8]{0:T(128)} %copy-done.9, s32[16]{0:T(128)} %select_reduce_fusion.1.slot_of, s32[2]{0:T(128)} %pad_add_fusion.1.half_ref, bf16[8,256,96]{2,1,0:T(8,128)(2,1)} %bitcast.40, bf16[4,2,8,256,96]{4,3,2,1,0:T(8,128)(2,1)} %bitcast.37, f32[8,1,512]{2,1,0:T(1,128)} %compare_convert_fusion.live_ref), custom_call_target="tpu_custom_call" | custom-call | flops 8000000000 | bytes 8000000 | tf_op jit(solution)/shard_map/attention/pallas_call | solution.py:134
  152.6 0.1 copy.29
  152.7 0.0 collective-permute-done
  152.7 0.9 broadcast_select_fusion.1.right_ref
  153.6 62.8 %mix.1 = (f32[64,3072]{1,0:T(8,128)}, bf16[64,3072]{1,0:T(8,128)(2,1)}, bf16[16,4,48,512]{3,2,1,0:T(8,128)(2,1)}) custom-call(bf16[2,4,4,64,96]{4,3,2,1,0:T(8,128)(2,1)} %bitcast.38, bf16[96,3072]{1,0:T(8,128)(2,1)} %broadcast_select_fusion.1.right_ref, bf16[64,3072]{1,0:T(8,128)(2,1)} %base_ref.1, f32[1,3072]{1,0:T(1,128)} %bitcast.39, ...), custom_call_target="tpu_custom_call" | custom-call | tf_op jit(solution)/shard_map/mix/pallas_call | solution.py:515
  216.4 45.8 %lift.1.left_ref = bf16[2,4,4,64,256]{4,3,2,1,0:T(8,128)(2,1)} custom-call(bf16[64,3072]{1,0:T(8,128)(2,1)} %get-tuple-element.23.x_ref, bf16[3072,512]{1,0:T(8,128)(2,1)} %bitcast.35), custom_call_target="tpu_custom_call" | custom-call | tf_op jit(solution)/shard_map/lift/pallas_call | solution.py:789
  262.2 0.0 collective-permute-done.2
  262.2 1.6 copy.33
  263.8 0.2 bitcast_select_fusion
  264.0 0.0 copy-start.10
  264.0 0.1 slice_bitcast_fusion
  264.1 1.0 copy.35
  265.0 1.0 copy.34
  266.0 0.0 collective-permute-done.1
  266.0 0.0 copy-done.10
  266.0 1.3 broadcast_select_fusion.right_ref
  267.3 55.0 %down.1 = bf16[64,3072]{1,0:T(8,128)(2,1)} custom-call(bf16[2,4,4,64,256]{4,3,2,1,0:T(8,128)(2,1)} %lift.1.left_ref, bf16[256,3072]{1,0:T(8,128)(2,1)} %broadcast_select_fusion.right_ref, f32[64,3072]{1,0:T(8,128)} %get-tuple-element.26.base_ref), custom_call_target="tpu_custom_call" | custom-call | tf_op jit(solution)/shard_map/down/pallas_call | solution.py:532
  322.4 1.8 copy.39
  (11 shorter events, 0.0 us)
Async XLA Ops:
  1.4 10.2 %copy-start.9 = (s32[8]{0:T(128)}, s32[8]{0:T(128)S(1)}, u32[]{:S(2)}) copy-start(s32[8]{0:T(128)S(1)} %get-tuple-element.37.own_map) | copy-start | bytes 100
  1.4 1.0 copy-start
  2.4 1.2 copy-start.3
  3.7 0.7 copy-start.7
  4.4 0.7 copy-start.8
  11.6 1.0 copy-start.1
  12.6 1.0 copy-start.2
  13.7 0.9 copy-start.4
  14.6 0.8 copy-start.5
  15.4 0.7 copy-start.6
  16.1 136.6 %collective-permute-start = (bf16[96,3072]{1,0:T(8,128)(2,1)S(1)}, bf16[96,3072]{1,0:T(8,128)(2,1)}, u32[]{:S(2)}, u32[]{:S(2)}) collective-permute-start(bf16[96,3072]{1,0:T(8,128)(2,1)S(1)} %get-tuple-element.21), channel_id=1, source_target_pairs={{1,96},{32,65},{65,32},{96,1},{3,98},{34,67},{67,34},{98,3},{5,100... | collective-permute-start | bytes 1769480 | tf_op jit(solution)/shard_map/ppermute | solution.py:981
  17.6 248.4 %collective-permute-start.1 = (bf16[256,3072]{1,0:T(8,128)(2,1)}, bf16[256,3072]{1,0:T(8,128)(2,1)}, u32[]{:S(2)}, u32[]{:S(2)}) collective-permute-start(bf16[256,3072]{1,0:T(8,128)(2,1)} %get-tuple-element.25), channel_id=1, source_target_pairs={{1,96},{32,65},{65,32},{96,1},{3,98},{34,67},{67,34},{98,3},{5,100... | collective-permute-start | bytes 4718600 | tf_op jit(solution)/shard_map/ppermute | solution.py:981
  110.0 4.2 %copy-start.12 = (s32[16]{0:T(128)S(1)}, s32[16]{0:T(128)}, u32[]{:S(2)}) copy-start(s32[16]{0:T(128)} %param.18) | copy-start | bytes 196
  110.0 4.9 %copy-start.11 = (s32[32]{0:T(128)S(1)}, s32[32]{0:T(128)}, u32[]{:S(2)}) copy-start(s32[32]{0:T(128)} %param.19) | copy-start | bytes 388
  110.7 151.6 %collective-permute-start.2 = (bf16[2,2048,96]{1,2,0:T(8,128)(2,1)S(1)}, bf16[2,2048,96]{1,2,0:T(8,128)(2,1)}, u32[]{:S(2)}, u32[]{:S(2)}) collective-permute-start(bf16[2,2048,96]{1,2,0:T(8,128)(2,1)S(1)} %copy.32), channel_id=1, source_target_pairs={{0,32},{33,1},{2,34},{35,3},{4,36},{37,5},{6,38},{39,7},{8,40},{41... | collective-permute-start | bytes 2359304 | tf_op jit(solution)/shard_map/ppermute | solution.py:1015
  264.0 2.0 copy-start.10

commit v6 on v5

--- a/solution.py
+++ b/solution.py
@@ -328,28 +328,36 @@
             )
     hand_over(2)
     hand_over(3)
+
+    def pass_on(half, side, quarter):
+        _, right, left, _ = rings[half]
+        two = pl.ds(2 * quarter, 2)
+        second[half, side, quarter] = go(
+            push(
+                held.at[half, 1 + side, two],
+                late.at[half, side, two],
+                sems[2],
+                (half * 2 + side) * 2 + quarter,
+                axes[half],
+                (right, left)[side],
+            )
+        )
+
+    for side in range(2):
+        for half in range(2):
+            step = 1 + side
+            swaps[half, step].wait_recv()
+            make(held.at[half, step], near.at[half, step], half, core, big_at(half, step))
+            pass_on(half, side, 1 - side)
     hook(0)
     for side in range(2):
         for half in range(2):
-            _, right, left, _ = rings[half]
-            step = 1 + side
-            swaps[half, step].wait_recv()
-            make(held.at[half, step], near.at[half, step], half, core, big_at(half, step))
             first[half, side].wait_recv()
-            part = held.at[half, step, pl.ds(2 * side, 2)]
+            part = held.at[half, 1 + side, pl.ds(2 * side, 2)]
             part[...] = (
                 part[...].astype(jnp.float32) + early[half, side].astype(jnp.float32)
             ).astype(jnp.bfloat16)
-            second[half, side] = go(
-                push(
-                    held.at[half, step],
-                    late.at[half, side],
-                    sems[2],
-                    half * 2 + side,
-                    axes[half],
-                    (right, left)[side],
-                )
-            )
+            pass_on(half, side, side)
     hook(1)
     for half in range(2):
         swaps[half, 3].wait_recv()
@@ -373,7 +381,8 @@
     for half in range(2):
         _, right, left, _ = rings[1 - half]
         for side in range(2):
-            second[half, side].wait_recv()
+            for quarter in range(2):
+                second[half, side, quarter].wait_recv()
         gather_small(half, 0)
         for side, peer in ((0, right), (1, left)):
             third[half, side] = go(
@@ -432,7 +441,7 @@
         pltpu.VMEM((2, 2, 16, width), jnp.bfloat16),
         pltpu.VMEM((2, 2, HALF, width), jnp.bfloat16),
         pltpu.VMEM((2, 3, HALF, width), jnp.bfloat16),
-    ] + [pltpu.SemaphoreType.DMA((n,)) for n in (8, 8, 4, 4, 4, 4, 4, 4, 4, 4)]
+    ] + [pltpu.SemaphoreType.DMA((n,)) for n in (8, 8, 4, 4, 8, 8, 4, 4, 4, 4)]
 
 
 def scatter_scope(left_ref, right_ref, scratch, finish, hook=lambda at: None):

time: 326 us -> 323 us (level); the launches traced: 324 us -> 325 us
    pallas_call x1, Pallas kernels: 62.8 us -> 80 us  [mix(): pl.pallas_call(mix_kernel, in_specs=[VM] * 5, out_specs=[VM] * 3, out_sha...]
    pallas_call x1, Pallas kernels: 36.9 us -> 22.5 us  [attention(): pl.pallas_call(attention_kernel, grid_spec=pltpu.PrefetchScalarGridSpec(n...]
  transfers between devices with their start and end apart: 3 -> 3, of which waited for: 0 -> 0; matrix products, arithmetic and copies ran while one was open for 3% -> 3% of each run, Pallas kernels for 72% -> 73%
where the time goes in v6:
time: 323 us; the launch traced here: 325 us
  Pallas kernels  297 us (92%)
  local copies, waits for them, and re-layouts  15.9 us (5%)
  starting transfers between devices  6.28 us (2%)
  other arithmetic  5.33 us (2%)
    pallas_call x1, Pallas kernels, project(): pl.pallas_call(project_kernel, in_specs=[VM] * 4, out_specs=[VM] * 2, out...  88.9 us
    pallas_call x1, Pallas kernels, mix(): pl.pallas_call(mix_kernel, in_specs=[VM] * 5, out_specs=[VM] * 3, out_sha...  80 us
    pallas_call x1, Pallas kernels, down(): pl.pallas_call(down_kernel, in_specs=[VM] * 3, out_specs=VM, out_shape=ja...  52.2 us
    pallas_call x1, Pallas kernels, lift(): pl.pallas_call(lift_kernel, in_specs=[VM] * 2, out_specs=VM, out_shape=ja...  46.4 us
    pallas_call x1, Pallas kernels, attention(): pl.pallas_call(attention_kernel, grid_spec=pltpu.PrefetchScalarGridSpec(n...  22.5 us
    unnamed x29, local copies, waits for them, and re-layouts  11.8 us
    pallas_call x1, Pallas kernels, prep(): pl.pallas_call(prep_kernel, grid_spec=pltpu.PrefetchScalarGridSpec(num_sc...  6.5 us
  transfers between devices with their start and end apart: 3, of which 0 were waited for; matrix products, arithmetic and copies ran while one was open for 3% of the time, Pallas kernels for 73%

profile of v6, /device:TPU:14, one launch (start us, length us, event | category | flops | bytes accessed | tf_op | source)
XLA Modules:
  0.0 324.9 jit_solution(14212364491818854607)
XLA Ops:
  0.6 0.7 add_multiply_fusion
  1.4 0.0 copy-start.9
  1.4 0.1 pad_add_fusion.2.place
  1.5 1.0 copy-done
  2.5 1.2 copy-done.3
  3.7 0.7 copy-done.7
  4.4 0.7 copy-done.8
  5.1 6.5 %prep.1 = (bf16[64,3072]{1,0:T(8,128)(2,1)S(1)}, bf16[16,48,384]{2,1,0:T(8,128)(2,1)S(1)}, bf16[16,48,512]{2,1,0:T(8,128)(2,1)S(1)}, bf16[96,3072]{1,0:T(8,128)(...) custom-call(s32[8]{0:T(128)S(1)} %get-tuple-element.37.own_map, ...), custom_call_target="tpu_custom_call" | custom-call | tf_op jit(solution)/shard_map/prep/pallas_call | solution.py:895
  11.6 0.0 copy-done.9
  11.6 1.0 copy-done.1
  12.6 1.0 copy-done.2
  13.7 0.9 copy-done.4
  14.6 0.8 copy-done.5
  15.4 0.7 copy-done.6
  16.1 1.5 collective-permute-start
  17.6 1.8 collective-permute-start.1
  19.5 88.9 %project.1 = (bf16[2,4,4,64,96]{4,3,2,1,0:T(8,128)(2,1)}, bf16[4,2,2,4,4,64,96]{6,5,4,3,2,1,0:T(8,128)(2,1)}) custom-call(bf16[64,3072]{1,0:T(8,128)(2,1)} %copy-done.6, bf16[16,48,384]{2,1,0:T(8,128)(2,1)} %copy-done.5, f32[2,4,4,64,96]{4,3,2,1,0:T(8,128)} %bitcast.31, f32[2,4,4,64,96]{4,3,2,1,0:T(8,128)} %bitcast.32), custom_call_target="tpu_custom_call" | custom-call | tf_op jit(solution)/shard_map/project/pallas_call | solution.py:779
  108.3 1.7 dynamic-slice_bitcast_fusion.1
  110.1 0.0 copy-start.12
  110.1 0.0 copy-start.11
  110.1 0.1 copy.31
  110.2 0.5 copy.32
  110.7 2.9 collective-permute-start.2
  113.6 0.6 pad_add_fusion.1.half_ref
  114.2 0.0 copy-done.12
  114.2 0.6 select_reduce_fusion.1.slot_of
  114.9 0.1 broadcast_add_fusion
  115.0 0.0 copy-done.11
  115.0 0.2 select_reduce_fusion
  115.1 0.6 compare_convert_fusion.live_ref
  115.8 22.5 %attention.1 = bf16[8,256,96]{2,1,0:T(8,128)(2,1)} custom-call(s32[8]{0:T(128)} %copy-done.9, s32[16]{0:T(128)} %select_reduce_fusion.1.slot_of, s32[2]{0:T(128)} %pad_add_fusion.1.half_ref, bf16[8,256,96]{2,1,0:T(8,128)(2,1)} %bitcast.40, bf16[4,2,8,256,96]{4,3,2,1,0:T(8,128)(2,1)} %bitcast.37, f32[8,1,512]{2,1,0:T(1,128)} %compare_convert_fusion.live_ref), custom_call_target="tpu_custom_call" | custom-call | flops 8000000000 | bytes 8000000 | tf_op jit(solution)/shard_map/attention/pallas_call | solution.py:134
  138.3 0.1 copy.29
  138.4 0.0 collective-permute-done
  138.4 0.9 broadcast_select_fusion.1.right_ref
  139.3 80.0 %mix.1 = (f32[64,3072]{1,0:T(8,128)}, bf16[64,3072]{1,0:T(8,128)(2,1)}, bf16[16,4,48,512]{3,2,1,0:T(8,128)(2,1)}) custom-call(bf16[2,4,4,64,96]{4,3,2,1,0:T(8,128)(2,1)} %bitcast.38, bf16[96,3072]{1,0:T(8,128)(2,1)} %broadcast_select_fusion.1.right_ref, bf16[64,3072]{1,0:T(8,128)(2,1)} %base_ref.1, f32[1,3072]{1,0:T(1,128)} %bitcast.39, ...), custom_call_target="tpu_custom_call" | custom-call | tf_op jit(solution)/shard_map/mix/pallas_call | solution.py:524
  219.3 46.4 %lift.1.left_ref = bf16[2,4,4,64,256]{4,3,2,1,0:T(8,128)(2,1)} custom-call(bf16[64,3072]{1,0:T(8,128)(2,1)} %get-tuple-element.23.x_ref, bf16[3072,512]{1,0:T(8,128)(2,1)} %bitcast.35), custom_call_target="tpu_custom_call" | custom-call | tf_op jit(solution)/shard_map/lift/pallas_call | solution.py:798
  265.8 0.0 collective-permute-done.2
  265.8 1.6 copy.33
  267.4 0.2 bitcast_select_fusion
  267.6 0.0 copy-start.10
  267.6 0.1 slice_bitcast_fusion
  267.7 1.0 copy.35
  268.6 1.0 copy.34
  269.6 0.0 collective-permute-done.1
  269.6 0.0 copy-done.10
  269.6 1.3 broadcast_select_fusion.right_ref
  270.9 52.2 %down.1 = bf16[64,3072]{1,0:T(8,128)(2,1)} custom-call(bf16[2,4,4,64,256]{4,3,2,1,0:T(8,128)(2,1)} %lift.1.left_ref, bf16[256,3072]{1,0:T(8,128)(2,1)} %broadcast_select_fusion.right_ref, f32[64,3072]{1,0:T(8,128)} %get-tuple-element.26.base_ref), custom_call_target="tpu_custom_call" | custom-call | tf_op jit(solution)/shard_map/down/pallas_call | solution.py:541
  323.1 1.8 copy.39
  (11 shorter events, 0.0 us)
Async XLA Ops:
  1.4 10.2 %copy-start.9 = (s32[8]{0:T(128)}, s32[8]{0:T(128)S(1)}, u32[]{:S(2)}) copy-start(s32[8]{0:T(128)S(1)} %get-tuple-element.37.own_map) | copy-start | bytes 100
  1.4 1.0 copy-start
  2.4 1.2 copy-start.3
  3.7 0.7 copy-start.7
  4.4 0.7 copy-start.8
  11.6 1.0 copy-start.1
  12.6 1.0 copy-start.2
  13.7 0.9 copy-start.4
  14.6 0.8 copy-start.5
  15.4 0.7 copy-start.6
  16.1 122.3 %collective-permute-start = (bf16[96,3072]{1,0:T(8,128)(2,1)S(1)}, bf16[96,3072]{1,0:T(8,128)(2,1)}, u32[]{:S(2)}, u32[]{:S(2)}) collective-permute-start(bf16[96,3072]{1,0:T(8,128)(2,1)S(1)} %get-tuple-element.21), channel_id=1, source_target_pairs={{1,96},{32,65},{65,32},{96,1},{3,98},{34,67},{67,34},{98,3},{5,100... | collective-permute-start | bytes 1769480 | tf_op jit(solution)/shard_map/ppermute | solution.py:990
  17.6 251.9 %collective-permute-start.1 = (bf16[256,3072]{1,0:T(8,128)(2,1)}, bf16[256,3072]{1,0:T(8,128)(2,1)}, u32[]{:S(2)}, u32[]{:S(2)}) collective-permute-start(bf16[256,3072]{1,0:T(8,128)(2,1)} %get-tuple-element.25), channel_id=1, source_target_pairs={{1,96},{32,65},{65,32},{96,1},{3,98},{34,67},{67,34},{98,3},{5,100... | collective-permute-start | bytes 4718600 | tf_op jit(solution)/shard_map/ppermute | solution.py:990
  110.1 4.2 %copy-start.12 = (s32[16]{0:T(128)S(1)}, s32[16]{0:T(128)}, u32[]{:S(2)}) copy-start(s32[16]{0:T(128)} %param.18) | copy-start | bytes 196
  110.1 4.9 %copy-start.11 = (s32[32]{0:T(128)S(1)}, s32[32]{0:T(128)}, u32[]{:S(2)}) copy-start(s32[32]{0:T(128)} %param.19) | copy-start | bytes 388
  110.7 155.1 %collective-permute-start.2 = (bf16[2,2048,96]{1,2,0:T(8,128)(2,1)S(1)}, bf16[2,2048,96]{1,2,0:T(8,128)(2,1)}, u32[]{:S(2)}, u32[]{:S(2)}) collective-permute-start(bf16[2,2048,96]{1,2,0:T(8,128)(2,1)S(1)} %copy.32), channel_id=1, source_target_pairs={{0,32},{33,1},{2,34},{35,3},{4,36},{37,5},{6,38},{39,7},{8,40},{41... | collective-permute-start | bytes 2359304 | tf_op jit(solution)/shard_map/ppermute | solution.py:1024
  267.6 2.0 copy-start.10
